TPU v7x, 32 devices: a whole 2x2x4 slice. The times are simulated.
32 devices in a mesh: group: 16 (over z, y, core), shard: 2 (over x).
Axes of the slice: x: 2, y: 2, z: 4, core: 2. Of those that a mesh axis runs over, the one named last changes fastest.
Arguments:
- frames: bfloat16 [64, 256, 512], P(('group', 'shard')), may hold values from -6 to 6
- lengths: int32 [64], P(('group', 'shard')), may hold values from 128 to 256, as said below
- cotangent: bfloat16 [64, 256, 512], P(('group', 'shard')), may hold values from -6 to 6
- ffn_in: float32 [2, 512, 2048], P(None, 'shard'), may hold values from -0.25 to 0.25
- ffn_in_moment: float32 [2, 512, 2048], P(None, 'shard'), may hold values from -10 to 10
- ffn_in_square: float32 [2, 512, 2048], P(None, 'shard'), may hold values from 0.2768896 to 1.1075584
- ffn_out: float32 [2, 2048, 512], P(None, 'shard'), may hold values from -0.25 to 0.25
- ffn_out_moment: float32 [2, 2048, 512], P(None, 'shard'), may hold values from -10 to 10
- ffn_out_square: float32 [2, 2048, 512], P(None, 'shard'), may hold values from 0.2768896 to 1.1075584
- attn_proj: float32 [4, 512, 512], P(None, 'shard')
- attn_moment: float32 [4, 512, 512], P(None, 'shard')
- attn_square: float32 [4, 512, 512], P(None, 'shard')
- conv_proj: float32 [512, 1536], P('shard')
- conv_moment: float32 [512, 1536], P('shard'), may hold values from -32 to 32
- conv_square: float32 [512, 1536], P('shard'), may hold values from 2.62144 to 10.48576
- vectors: float32 [37, 512], P(None, 'shard')
- vectors_moment: float32 [37, 512], P(None, 'shard'), may hold values from -32 to 32
- vectors_square: float32 [37, 512], P(None, 'shard'), may hold values from 2.62144 to 10.48576
- rel_keys: float32 [73, 64], replicated, may hold values from -4 to 4
- rel_moment: float32 [73, 64], replicated, may hold values from -40 to 40
- rel_square: float32 [73, 64], replicated, may hold values from 4.096 to 16.384
Outputs:
- output: bfloat16 [64, 256, 512], P(('group', 'shard'))
- input_grad: bfloat16 [64, 256, 512], P(('group', 'shard'))
- grad_ffn_in: float32 [2, 512, 2048], P(None, 'shard')
- new_ffn_in: float32 [2, 512, 2048], P(None, 'shard')
- new_ffn_in_moment: float32 [2, 512, 2048], P(None, 'shard')
- new_ffn_in_square: float32 [2, 512, 2048], P(None, 'shard')
- grad_ffn_out: float32 [2, 2048, 512], P(None, 'shard')
- new_ffn_out: float32 [2, 2048, 512], P(None, 'shard')
- new_ffn_out_moment: float32 [2, 2048, 512], P(None, 'shard')
- new_ffn_out_square: float32 [2, 2048, 512], P(None, 'shard')
- grad_attn_proj: float32 [4, 512, 512], P(None, 'shard')
- new_attn_proj: float32 [4, 512, 512], P(None, 'shard')
- new_attn_moment: float32 [4, 512, 512], P(None, 'shard')
- new_attn_square: float32 [3, 512, 512], P(None, 'shard')
- new_attn_out_square: float32 [512, 512], P('shard')
- grad_conv_proj: float32 [512, 1536], P('shard')
- new_conv_proj: float32 [512, 1536], P('shard')
- new_conv_moment: float32 [512, 1536], P('shard')
- new_conv_square: float32 [512, 1536], P('shard')
- grad_vectors: float32 [37, 512], P(None, 'shard')
- new_vectors: float32 [37, 512], P(None, 'shard')
- new_vectors_moment: float32 [37, 512], P(None, 'shard')
- new_vectors_square: float32 [37, 512], P(None, 'shard')
- grad_rel_keys: float32 [73, 64], replicated
- new_rel_keys: float32 [73, 64], replicated
- new_rel_moment: float32 [73, 64], replicated
- new_rel_square: float32 [73, 64], replicated
- trust_norms: float32 [2, 18], replicated
Inputs may be any that keep to these rules, and one draw needn't show every extreme that they name: `lengths`: every sequence has at least 128 valid frames; the first sequence has all 256.
All inputs are finite; a program needn't handle non-finite values.
Results may differ from a plain program's by a relative error of at most 0.02.
Values may be sent and summed in bfloat16 or wider, within the bound.
No kernel may reach another device: no remote copies, remote signals or barrier semaphores. Data moves between devices by JAX's collectives and lax.ppermute only.
A program may use at most 320 MiB of HBM per device.

v0:
```python
import math

import jax
import jax.numpy as jnp
from jax import lax
from jax.sharding import PartitionSpec as P

D = 512
HEADS = 8
KERNEL = 31
BACK = 64
STEP = 10


NORM_EPSILON = 1e-05
ADAM_EPSILON = 1e-06
RATIO_EPSILON = 1e-06
BETA_FIRST = 0.9
BETA_SECOND = 0.999
WEIGHT_DECAY = 0.01
LEARN_RATE = 0.5
MASKED_SCORE = -1e30


def product(left_side, right_side):
    return jnp.dot(left_side, right_side, preferred_element_type=jnp.float32)


def contract_rows(left_side, right_side):
    return lax.dot_general(
        left_side, right_side, (((0,), (0,)), ((), ())), preferred_element_type=jnp.float32
    )


def contract_cols(left_side, right_side):
    return lax.dot_general(
        left_side, right_side, (((1,), (1,)), ((), ())), preferred_element_type=jnp.float32
    )


def layer_stats(values):
    centred = values - jnp.mean(values, axis=-1, keepdims=True)
    norm_scale = lax.rsqrt(jnp.mean(centred * centred, axis=-1, keepdims=True) + NORM_EPSILON)
    return (centred * norm_scale, norm_scale)


def norm_back(grad_out, normed, norm_scale, gain_row):
    grad_gain = jnp.sum(grad_out * normed, axis=0)
    scaled = grad_out * gain_row
    row_inner = jnp.mean(scaled * normed, axis=-1, keepdims=True)
    grad_in = norm_scale * (scaled - jnp.mean(scaled, axis=-1, keepdims=True) - normed * row_inner)
    return (grad_in, grad_gain)


def swish_slope(before):
    logistic = jax.nn.sigmoid(before)
    return logistic * (1.0 + before * (1.0 - logistic))


def feed_forward(values, gain_row, weight_in, weight_out):
    normed, norm_scale = layer_stats(values)
    entry_low = (normed * gain_row).astype(jnp.bfloat16)
    before = product(entry_low, weight_in)
    hidden = jax.nn.silu(before).astype(jnp.bfloat16)
    return (product(hidden, weight_out), (normed, norm_scale, entry_low, before, hidden))


def feed_back(grad_res, kept_state, gain_row, weight_in, weight_out):
    normed, norm_scale, entry_low, before, hidden = kept_state
    grad_branch = (0.5 * grad_res).astype(jnp.bfloat16)
    grad_out_weight = contract_rows(hidden, grad_branch)
    grad_hidden = contract_cols(grad_branch, weight_out)
    grad_before = (grad_hidden * swish_slope(before)).astype(jnp.bfloat16)
    grad_in_weight = contract_rows(entry_low, grad_before)
    grad_entry = contract_cols(grad_before, weight_in)
    grad_input, grad_gain = norm_back(grad_entry, normed, norm_scale, gain_row)
    return (grad_res + grad_input, grad_gain, grad_in_weight, grad_out_weight)


def band_bias(relative, row_start, key_count):
    head_count, row_count, rel_count = relative.shape
    width = key_count + row_count
    lead = row_count - 1 + row_start - BACK
    pieces = [jnp.broadcast_to(relative[:, :, :1], (head_count, row_count, lead)), relative]
    used = lead + rel_count
    pieces.append(
        jnp.broadcast_to(relative[:, :, rel_count - 1 :], (head_count, row_count, width - used))
    )
    table = jnp.concatenate(pieces, axis=2)[:, :, :width]
    flat = table.reshape(head_count, row_count * width)
    skewed = flat[:, row_count - 1 : row_count - 1 + row_count * (width - 1)].reshape(
        head_count, row_count, width - 1
    )
    return skewed[:, :, :key_count]


def block_scores(query_block, key_heads, rel_weights, row_start, length):
    row_count, head_count, head_width = query_block.shape
    key_count = key_heads.shape[0]
    raw_scores = jnp.einsum(
        "ihe,jhe->hij", query_block, key_heads, preferred_element_type=jnp.float32
    )
    relative = jnp.einsum(
        "ihe,re->hir", query_block, rel_weights, preferred_element_type=jnp.float32
    )
    scores = (raw_scores + band_bias(relative, row_start, key_count)) * (
        1.0 / math.sqrt(head_width)
    )
    valid = jnp.arange(key_count) < length
    return jnp.where(valid[None, None, :], scores, MASKED_SCORE)


def spread_back(grad_bias, row_start, rel_count):
    empty_table = jnp.zeros((grad_bias.shape[0], grad_bias.shape[1], rel_count), jnp.float32)
    pullback = jax.vjp(
        lambda relative: band_bias(relative, row_start, grad_bias.shape[2]), empty_table
    )[1]
    return pullback(grad_bias)[0]


def attend_forward(entry_low, attn_weights, rel_weights, length):
    row_count, feat_width = entry_low.shape
    triple = jnp.einsum(
        "td,kde->kte", entry_low, attn_weights[:3], preferred_element_type=jnp.float32
    )
    triple = triple.astype(jnp.bfloat16).reshape(3, row_count, HEADS, feat_width // HEADS)
    query_heads, key_heads, value_heads = (triple[0], triple[1], triple[2])
    scores = block_scores(query_heads, key_heads, rel_weights, 0, length)
    row_max = jnp.max(scores, axis=-1, keepdims=True)
    log_total = row_max + jnp.log(jnp.sum(jnp.exp(scores - row_max), axis=-1, keepdims=True))
    prob_low = jnp.exp(scores - log_total).astype(jnp.bfloat16)
    mixed_parts = jnp.einsum(
        "hij,jhe->ihe", prob_low, value_heads, preferred_element_type=jnp.float32
    )
    log_totals = [log_total]
    mixed_low = mixed_parts.astype(jnp.bfloat16).reshape(row_count, feat_width)
    return (mixed_low, (query_heads, key_heads, value_heads, log_totals))


def attend_back(grad_mixed, kept_state, rel_weights, length):
    query_heads, key_heads, value_heads, log_totals = kept_state
    row_count, head_count, head_width = query_heads.shape
    block_rows = min(row_count, 512)
    norm_factor = 1.0 / math.sqrt(head_width)
    grad_keys = jnp.zeros(query_heads.shape, jnp.float32)
    grad_values = jnp.zeros(query_heads.shape, jnp.float32)
    grad_rel = jnp.zeros(rel_weights.shape, jnp.float32)
    query_parts = []
    for block_index, row_start in enumerate(range(0, row_count, block_rows)):
        scores = block_scores(query_heads, key_heads, rel_weights, row_start, length)
        prob_full = jnp.exp(scores - log_totals[block_index])
        grad_values = jnp.einsum(
            "hij,ihe->jhe",
            prob_full.astype(jnp.bfloat16),
            grad_mixed,
            preferred_element_type=jnp.float32,
        )
        grad_probs = jnp.einsum(
            "ihe,jhe->hij", grad_mixed, value_heads, preferred_element_type=jnp.float32
        )
        row_inner = jnp.sum(prob_full * grad_probs, axis=-1, keepdims=True)
        grad_scores = (prob_full * (grad_probs - row_inner)).astype(jnp.bfloat16)
        grad_query = (
            jnp.einsum("hij,jhe->ihe", grad_scores, key_heads, preferred_element_type=jnp.float32)
            * norm_factor
        )
        grad_keys = (
            jnp.einsum("hij,ihe->jhe", grad_scores, query_heads, preferred_element_type=jnp.float32)
            * norm_factor
        )
        grad_relative = spread_back(
            grad_scores.astype(jnp.float32) * norm_factor, row_start, rel_weights.shape[0]
        ).astype(jnp.bfloat16)
        query_parts.append(
            grad_query
            + jnp.einsum(
                "hir,re->ihe", grad_relative, rel_weights, preferred_element_type=jnp.float32
            )
        )
        grad_rel = jnp.einsum(
            "hir,ihe->re", grad_relative, query_heads, preferred_element_type=jnp.float32
        )
    return (query_parts[0], grad_keys, grad_values, grad_rel)


def conv_forward(values, gain_outer, gain_inner, depth_taps, conv_weights):
    row_count, feat_width = values.shape
    normed, norm_scale = layer_stats(values)
    entry_low = (normed * gain_outer).astype(jnp.bfloat16)
    both_halves = product(entry_low, conv_weights[:, : 2 * feat_width])
    linear = both_halves[:, :feat_width]
    gate_sig = jax.nn.sigmoid(both_halves[:, feat_width:])
    padded = jnp.pad(linear * gate_sig, ((KERNEL - 1, 0), (0, 0)))
    conved = depth_taps[0] * padded[0:row_count]
    for offset in range(1, KERNEL):
        conved = conved + depth_taps[offset] * padded[offset : offset + row_count]
    inner_normed, inner_scale = layer_stats(conved)
    act_in = inner_normed * gain_inner
    act_low = jax.nn.silu(act_in).astype(jnp.bfloat16)
    branch_out = product(act_low, conv_weights[:, 2 * feat_width :])
    return (
        branch_out,
        (
            normed,
            norm_scale,
            entry_low,
            linear,
            gate_sig,
            padded,
            inner_normed,
            inner_scale,
            act_in,
            act_low,
        ),
    )


def conv_back(grad_res, kept_state, gain_outer, gain_inner, depth_taps, conv_weights):
    (
        normed,
        norm_scale,
        entry_low,
        linear,
        gate_sig,
        padded,
        inner_normed,
        inner_scale,
        act_in,
        act_low,
    ) = kept_state
    row_count, feat_width = linear.shape
    grad_branch = grad_res.astype(jnp.bfloat16)
    grad_second = contract_rows(act_low, grad_branch)
    grad_act = contract_cols(grad_branch, conv_weights[:, 2 * feat_width :]) * swish_slope(act_in)
    grad_conved, grad_gain_inner = norm_back(grad_act, inner_normed, inner_scale, gain_inner)
    grad_taps = jnp.stack(
        [
            jnp.sum(grad_conved * padded[offset : offset + row_count], axis=0)
            for offset in range(KERNEL)
        ]
    )
    grad_pad = jnp.pad(grad_conved, ((0, KERNEL - 1), (0, 0)))
    grad_gated = depth_taps[0] * grad_pad[KERNEL - 1 : KERNEL - 1 + row_count]
    for offset in range(1, KERNEL):
        grad_gated = (
            grad_gated
            + depth_taps[offset] * grad_pad[KERNEL - 1 - offset : KERNEL - 1 - offset + row_count]
        )
    grad_both = jnp.concatenate(
        [grad_gated * gate_sig, grad_gated * linear * gate_sig * (1.0 - gate_sig)], axis=1
    ).astype(jnp.bfloat16)
    grad_first = contract_rows(entry_low, grad_both)
    grad_entry = contract_cols(grad_both, conv_weights[:, : 2 * feat_width])
    grad_input, grad_gain_outer = norm_back(grad_entry, normed, norm_scale, gain_outer)
    return (
        grad_res + grad_input,
        grad_gain_outer,
        grad_gain_inner,
        grad_taps,
        jnp.concatenate([grad_first, grad_second], axis=1),
    )


def one_sequence(frame_low, length, cot_row, weights, rel_weights):
    weight_in, weight_out, attn_weights, conv_weights, vec_low = weights
    vec_full = vec_low.astype(jnp.float32)
    depth_taps = vec_full[:KERNEL]
    gain_rows = vec_full[KERNEL:]
    stream_in = frame_low.astype(jnp.float32)
    branch_one, kept_one = feed_forward(stream_in, gain_rows[0], weight_in[0], weight_out[0])
    after_ffn = stream_in + 0.5 * branch_one
    attn_normed, attn_scale = layer_stats(after_ffn)
    attn_entry = (attn_normed * gain_rows[1]).astype(jnp.bfloat16)
    mixed_low, kept_attn = attend_forward(attn_entry, attn_weights, rel_weights, length)
    after_attn = after_ffn + product(mixed_low, attn_weights[3])
    conv_branch, kept_conv = conv_forward(
        after_attn, gain_rows[2], gain_rows[3], depth_taps, conv_weights
    )
    after_conv = after_attn + conv_branch
    branch_two, kept_two = feed_forward(after_conv, gain_rows[4], weight_in[1], weight_out[1])
    after_last = after_conv + 0.5 * branch_two
    final_normed, final_scale = layer_stats(after_last)
    output_row = (final_normed * gain_rows[5]).astype(jnp.bfloat16)
    valid = (jnp.arange(frame_low.shape[0]) < length)[:, None]
    grad_top = jnp.where(valid, cot_row.astype(jnp.float32), 0.0)
    grad_last, gain_grad_five = norm_back(grad_top, final_normed, final_scale, gain_rows[5])
    grad_conv_in, gain_grad_four, grad_in_two, grad_out_two = feed_back(
        grad_last, kept_two, gain_rows[4], weight_in[1], weight_out[1]
    )
    grad_attn_in, gain_grad_two, gain_grad_three, grad_taps, grad_conv_weight = conv_back(
        grad_conv_in, kept_conv, gain_rows[2], gain_rows[3], depth_taps, conv_weights
    )
    grad_attn_low = grad_attn_in.astype(jnp.bfloat16)
    grad_out_proj = contract_rows(mixed_low, grad_attn_low)
    grad_mixed = (
        contract_cols(grad_attn_low, attn_weights[3])
        .astype(jnp.bfloat16)
        .reshape(kept_attn[0].shape)
    )
    grad_queries, grad_keys, grad_values, grad_rel = attend_back(
        grad_mixed, kept_attn, rel_weights, length
    )
    grad_triple = (
        jnp.stack([grad_queries, grad_keys, grad_values])
        .astype(jnp.bfloat16)
        .reshape(3, frame_low.shape[0], frame_low.shape[1])
    )
    grad_proj = jnp.einsum(
        "td,kte->kde", attn_entry, grad_triple, preferred_element_type=jnp.float32
    )
    grad_entry = jnp.einsum(
        "kte,kde->td", grad_triple, attn_weights[:3], preferred_element_type=jnp.float32
    )
    grad_norm_in, gain_grad_one = norm_back(grad_entry, attn_normed, attn_scale, gain_rows[1])
    grad_after_ffn = grad_attn_in + grad_norm_in
    grad_stream, gain_grad_zero, grad_in_one, grad_out_one = feed_back(
        grad_after_ffn, kept_one, gain_rows[0], weight_in[0], weight_out[0]
    )
    gain_grads = jnp.stack(
        [
            gain_grad_zero,
            gain_grad_one,
            gain_grad_two,
            gain_grad_three,
            gain_grad_four,
            gain_grad_five,
        ]
    )
    local_grads = (
        jnp.stack([grad_in_one, grad_in_two]),
        jnp.stack([grad_out_one, grad_out_two]),
        jnp.concatenate([grad_proj, grad_out_proj[None]], axis=0),
        grad_conv_weight,
        jnp.concatenate([grad_taps, gain_grads], axis=0),
        grad_rel,
    )
    return (output_row, grad_stream.astype(jnp.bfloat16), local_grads)


def owner_flat(values, dim_index, shards):
    layout = values.shape
    blocked = layout[:dim_index] + (shards, layout[dim_index] // shards) + layout[dim_index + 1 :]
    return jnp.moveaxis(values.reshape(blocked), dim_index, 0).reshape(shards, -1)


def adam_update(weight, moment, square, grad_sum):
    new_moment = BETA_FIRST * moment + (1.0 - BETA_FIRST) * grad_sum
    new_square = BETA_SECOND * square + (1.0 - BETA_SECOND) * grad_sum * grad_sum
    first_hat = new_moment / (1.0 - BETA_FIRST**STEP)
    second_hat = new_square / (1.0 - BETA_SECOND**STEP)
    update = first_hat / (jnp.sqrt(second_hat) + ADAM_EPSILON) + WEIGHT_DECAY * weight
    return (new_moment, new_square, update)


def unit_sums(ffn_in_part, ffn_out_part, attn_part, conv_part, vector_part):
    return jnp.concatenate(
        [
            jnp.sum(ffn_in_part * ffn_in_part, axis=(1, 2)),
            jnp.sum(ffn_out_part * ffn_out_part, axis=(1, 2)),
            jnp.sum(attn_part * attn_part, axis=(1, 2)),
            jnp.stack(
                [
                    jnp.sum(conv_part[:, : 2 * D] * conv_part[:, : 2 * D]),
                    jnp.sum(conv_part[:, 2 * D :] * conv_part[:, 2 * D :]),
                ]
            ),
            jnp.sum(vector_part[:KERNEL] * vector_part[:KERNEL])[None],
            jnp.sum(vector_part[KERNEL:] * vector_part[KERNEL:], axis=1),
        ]
    )


def apply_ratios(masters, updates, ratios):
    conv_factor = jnp.where(jnp.arange(3 * D) < 2 * D, ratios[8], ratios[9])[None, :]
    vector_factor = jnp.concatenate([jnp.full((KERNEL,), ratios[10]), ratios[11:17]])[:, None]
    factors = (
        ratios[0:2][:, None, None],
        ratios[2:4][:, None, None],
        ratios[4:8][:, None, None],
        conv_factor,
        vector_factor,
    )
    return tuple(
        (
            weight - LEARN_RATE * factor * update
            for weight, factor, update in zip(masters, factors, updates)
        )
    )


def body(
    frames,
    lengths,
    cotangent,
    ffn_in,
    ffn_in_moment,
    ffn_in_square,
    ffn_out,
    ffn_out_moment,
    ffn_out_square,
    attn_proj,
    attn_moment,
    attn_square,
    conv_proj,
    conv_moment,
    conv_square,
    vectors,
    vectors_moment,
    vectors_square,
    rel_keys,
    rel_moment,
    rel_square,
):
    rel_weights = rel_keys.astype(jnp.bfloat16)
    outputs = []
    input_grads = []
    totals = None
    for sequence in range(frames.shape[0]):
        weights = (
            lax.all_gather(ffn_in.astype(jnp.bfloat16), "shard", axis=1, tiled=True),
            lax.all_gather(ffn_out.astype(jnp.bfloat16), "shard", axis=1, tiled=True),
            lax.all_gather(attn_proj.astype(jnp.bfloat16), "shard", axis=1, tiled=True),
            lax.all_gather(conv_proj.astype(jnp.bfloat16), "shard", axis=0, tiled=True),
            lax.all_gather(vectors.astype(jnp.bfloat16), "shard", axis=1, tiled=True),
        )
        output_row, input_row, local_grads = one_sequence(
            frames[sequence], lengths[sequence], cotangent[sequence], weights, rel_weights
        )
        outputs.append(output_row)
        input_grads.append(input_row)
        if totals is None:
            totals = local_grads
        else:
            totals = tuple(
                (left_part + right_part for left_part, right_part in zip(totals, local_grads))
            )
    masters = (ffn_in, ffn_out, attn_proj, conv_proj, vectors)
    rel_grad = lax.psum(totals[5], ("group", "shard"))
    shards = lax.axis_size("shard")
    groups = lax.axis_size("group")
    shard_dims = (1, 1, 1, 0, 1)
    lined = jnp.concatenate(
        [owner_flat(totals[index], shard_dims[index], shards) for index in range(5)], axis=1
    )
    owned_count = lined.shape[1]
    spread = jnp.swapaxes(lined.reshape(shards, groups, owned_count // groups), 0, 1).reshape(-1)
    reduced_piece = lax.psum_scatter(spread, ("group", "shard"), scatter_dimension=0, tiled=True)
    owned_flat = lax.all_gather(
        reduced_piece.astype(jnp.bfloat16), "group", axis=0, tiled=True
    ).astype(reduced_piece.dtype)
    pieces = []
    offset = 0
    for master in masters:
        pieces.append(owned_flat[offset : offset + master.size].reshape(master.shape))
        offset = offset + master.size
    owned_grads = tuple(pieces)
    moments = (ffn_in_moment, ffn_out_moment, attn_moment, conv_moment, vectors_moment)
    squares = (ffn_in_square, ffn_out_square, attn_square, conv_square, vectors_square)
    states = [
        adam_update(weight, moment, square, grad_sum)
        for weight, moment, square, grad_sum in zip(masters, moments, squares, owned_grads)
    ]
    updates = tuple((state[2] for state in states))
    weight_sums = unit_sums(masters[0], masters[1], masters[2], masters[3], masters[4])
    update_sums = unit_sums(updates[0], updates[1], updates[2], updates[3], updates[4])
    norm_totals = lax.psum(jnp.stack([weight_sums, update_sums]), "shard")
    rel_moment_new, rel_square_new, rel_update = adam_update(
        rel_keys, rel_moment, rel_square, rel_grad
    )
    all_sums = jnp.concatenate(
        [
            norm_totals,
            jnp.stack([jnp.sum(rel_keys * rel_keys), jnp.sum(rel_update * rel_update)])[:, None],
        ],
        axis=1,
    )
    trust_norms = jnp.sqrt(all_sums)
    ratios = trust_norms[0] / jnp.sqrt(all_sums[1] + RATIO_EPSILON)
    new_masters = apply_ratios(masters, updates, ratios)
    new_rel = rel_keys - LEARN_RATE * ratios[17] * rel_update
    return (
        jnp.stack(outputs),
        jnp.stack(input_grads),
        owned_grads[0],
        new_masters[0],
        states[0][0],
        states[0][1],
        owned_grads[1],
        new_masters[1],
        states[1][0],
        states[1][1],
        owned_grads[2],
        new_masters[2],
        states[2][0],
        states[2][1][:3],
        states[2][1][3],
        owned_grads[3],
        new_masters[3],
        states[3][0],
        states[3][1],
        owned_grads[4],
        new_masters[4],
        states[4][0],
        states[4][1],
        rel_grad,
        new_rel,
        rel_moment_new,
        rel_square_new,
        trust_norms,
    )


def solution(mesh):
    return jax.shard_map(
        body,
        mesh=mesh,
        in_specs=(
            P(("group", "shard"), None, None),
            P(("group", "shard")),
            P(("group", "shard"), None, None),
            P(None, "shard", None),
            P(None, "shard", None),
            P(None, "shard", None),
            P(None, "shard", None),
            P(None, "shard", None),
            P(None, "shard", None),
            P(None, "shard", None),
            P(None, "shard", None),
            P(None, "shard", None),
            P("shard", None),
            P("shard", None),
            P("shard", None),
            P(None, "shard"),
            P(None, "shard"),
            P(None, "shard"),
            P(),
            P(),
            P(),
        ),
        out_specs=(
            P(("group", "shard"), None, None),
            P(("group", "shard"), None, None),
            P(None, "shard", None),
            P(None, "shard", None),
            P(None, "shard", None),
            P(None, "shard", None),
            P(None, "shard", None),
            P(None, "shard", None),
            P(None, "shard", None),
            P(None, "shard", None),
            P(None, "shard", None),
            P(None, "shard", None),
            P(None, "shard", None),
            P(None, "shard", None),
            P("shard", None),
            P("shard", None),
            P("shard", None),
            P("shard", None),
            P("shard", None),
            P(None, "shard"),
            P(None, "shard"),
            P(None, "shard"),
            P(None, "shard"),
            P(),
            P(),
            P(),
            P(),
            P(),
        ),
        check_vma=False,
    )
```

profile of v0, /device:TPU:0, one launch (start us, length us, event | category | flops | bytes accessed | tf_op | source)
XLA Modules:
  0.0 1516.3 jit_solution(11446137562784984711)
XLA Ops:
  19.0 5.4 all_gather.23
  31.7 39.0 %all-gather.5.cloned.1.call-done = bf16[2,512,2048]{2,1,0:T(8,128)(2,1)} async-done(((bf16[2,256,2048]{2,1,0:T(8,128)(2,1)}), bf16[2,512,2048]{2,1,0:T(8,128)(2,1)}) %all-gather.5.cloned.1.call-update) | async-done | bytes 4194320 | tf_op jit(solution)/shard_map/all_gather | solution.py:420
  73.1 56.7 %all-gather.7.cloned.1.call-done = bf16[2,2048,512]{2,1,0:T(8,128)(2,1)} async-done(((bf16[2,1024,512]{2,1,0:T(8,128)(2,1)}), bf16[2,2048,512]{2,1,0:T(8,128)(2,1)}) %all-gather.7.cloned.1.call-update) | async-done | bytes 4194320 | tf_op jit(solution)/shard_map/all_gather | solution.py:421
  132.5 32.6 %all-gather.9.cloned.1.call-done = bf16[4,512,512]{2,1,0:T(8,128)(2,1)} async-done(((bf16[4,256,512]{2,1,0:T(8,128)(2,1)}), bf16[4,512,512]{2,1,0:T(8,128)(2,1)}) %all-gather.9.cloned.1.call-update) | async-done | bytes 2097168 | tf_op jit(solution)/shard_map/all_gather | solution.py:422
  174.2 8.2 reshape.736
  224.2 8.0 reshape.739
  298.9 6.4 reshape.745
  330.2 6.4 reshape.742
  418.2 6.4 add.908
  429.6 5.2 copy.291
  438.6 16.5 %copy.290 = f32[1,2,2048,512]{3,1,2,0:T(2,128)} copy(f32[1,2,2048,512]{3,2,1,0:T(8,128)S(1)} %bitcast.536) | data formatting | bytes 16777216
  465.7 7.3 copy.289
  489.5 53.2 %reshape.781 = f32[6048256]{0:T(1024)} reshape(f32[2,3024128]{1,0:T(2,128)} %constant_dynamic-update-slice_fusion) | data formatting | bytes 48386048
  542.6 29.5 %reshape.755 = f32[2,16,189008]{2,1,0:T(8,128)} reshape(f32[6048256]{0:T(1024)} %reshape.781) | data formatting | bytes 48386048 | tf_op jit(solution)/shard_map/reshape | solution.py:446
  572.2 34.6 %copy.300 = f32[2,16,189008]{2,0,1:T(2,128)} copy(f32[2,16,189008]{2,1,0:T(8,128)} %reshape.755) | data formatting | bytes 48386048 | tf_op jit(solution)/shard_map/reshape | solution.py:446
  606.7 272.0 %while.1 = (u32[]{:T(128)}, f32[16,2,189008]{2,1,0:T(2,128)}, f32[6048256]{0:T(1024)}, u32[]{}, u32[]{}, /*index=5*/u32[]{}, u32[]{}) while((u32[]{:T(128)}, f32[16,2,189008]{2,1,0:T(2,128)}, f32[6048256]{0:T(1024)}, u32[]{}, u32[]{}, /*index=5*/u32[]{}, u32[]{}) %tuple.225), condition=%wide.cond, body=%wide.body.sunk | while | flops 9 | bytes 18144940
  615.4 25.3 %dynamic-update-slice.13 = f32[6048256]{0:T(1024)} dynamic-update-slice(f32[6048256]{0:T(1024)} %get-tuple-element.319, f32[756032]{0:T(1024)S(1)} %reshape.785, u32[]{:T(128)S(6)} %add.2602) | dynamic-update-slice | bytes 6048260
  649.3 25.4 %dynamic-update-slice.13 = f32[6048256]{0:T(1024)} dynamic-update-slice(f32[6048256]{0:T(1024)} %get-tuple-element.319, f32[756032]{0:T(1024)S(1)} %reshape.785, u32[]{:T(128)S(6)} %add.2602) | dynamic-update-slice | bytes 6048260
  683.4 25.4 %dynamic-update-slice.13 = f32[6048256]{0:T(1024)} dynamic-update-slice(f32[6048256]{0:T(1024)} %get-tuple-element.319, f32[756032]{0:T(1024)S(1)} %reshape.785, u32[]{:T(128)S(6)} %add.2602) | dynamic-update-slice | bytes 6048260
  717.4 25.4 %dynamic-update-slice.13 = f32[6048256]{0:T(1024)} dynamic-update-slice(f32[6048256]{0:T(1024)} %get-tuple-element.319, f32[756032]{0:T(1024)S(1)} %reshape.785, u32[]{:T(128)S(6)} %add.2602) | dynamic-update-slice | bytes 6048260
  751.4 25.4 %dynamic-update-slice.13 = f32[6048256]{0:T(1024)} dynamic-update-slice(f32[6048256]{0:T(1024)} %get-tuple-element.319, f32[756032]{0:T(1024)S(1)} %reshape.785, u32[]{:T(128)S(6)} %add.2602) | dynamic-update-slice | bytes 6048260
  785.5 25.4 %dynamic-update-slice.13 = f32[6048256]{0:T(1024)} dynamic-update-slice(f32[6048256]{0:T(1024)} %get-tuple-element.319, f32[756032]{0:T(1024)S(1)} %reshape.785, u32[]{:T(128)S(6)} %add.2602) | dynamic-update-slice | bytes 6048260
  819.5 25.4 %dynamic-update-slice.13 = f32[6048256]{0:T(1024)} dynamic-update-slice(f32[6048256]{0:T(1024)} %get-tuple-element.319, f32[756032]{0:T(1024)S(1)} %reshape.785, u32[]{:T(128)S(6)} %add.2602) | dynamic-update-slice | bytes 6048260
  853.6 25.1 %dynamic-update-slice.13 = f32[6048256]{0:T(1024)} dynamic-update-slice(f32[6048256]{0:T(1024)} %get-tuple-element.319, f32[756032]{0:T(1024)S(1)} %reshape.785, u32[]{:T(128)S(6)} %add.2602) | dynamic-update-slice | bytes 6048260
  880.0 392.3 %all-reduce.20 = (bf16[6048256]{0:T(1024)(128)(2,1)}, f32[73,64]{0,1:T(8,128)S(1)}) all-reduce(f32[6048256]{0:T(1024)} %get-tuple-element.32, f32[73,64]{0,1:T(8,128)S(1)} %fusion.41), channel_id=2, replica_groups=mesh['group'=16,'shard'=2] {'group','shard'}, use_global_device_ids=true, to_apply=%region_132.133.clone | all-reduce | flops 6052928 | bytes 36326912
  1276.5 6.7 dynamic-update-slice
  1293.6 124.0 %all-reduce.19.cloned.1.call-done = bf16[3024128]{0:T(1024)(128)(2,1)} async-done(((bf16[3024128]{0:T(1024)(128)(2,1)}), bf16[3024128]{0:T(1024)(128)(2,1)}) %all-reduce.19.cloned.1.call-update) | async-done | bytes 6048272
  1429.1 6.2 fusion.335
  1450.5 11.2 multiply_reduce_fusion.2
  1464.2 7.3 multiply_reduce_fusion.3
  1479.2 5.2 psum.14
  1502.9 6.4 multiply_subtract_fusion.1
  (1018 shorter events, 418.8 us)
Async XLA Ops:
  7.2 63.5 %all-gather.5.cloned.1.call-start = ((), (), s32[]{:S(2)}) async-start(), calls=%async_computation | async-start | bytes 6291456 | tf_op jit(solution)/shard_map/all_gather | solution.py:420
  11.1 118.7 %all-gather.7.cloned.1.call-start = ((), (), s32[]{:S(2)}) async-start(), calls=%async_computation.1 | async-start | bytes 6291456 | tf_op jit(solution)/shard_map/all_gather | solution.py:421
  15.0 150.1 %all-gather.9.cloned.1.call-start = ((), (), s32[]{:S(2)}) async-start(), calls=%async_computation.2 | async-start | bytes 3145728 | tf_op jit(solution)/shard_map/all_gather | solution.py:422
  17.9 184.9 %all-gather.11.cloned.1.call-start = ((), (), s32[]{:S(2)}) async-start(), calls=%async_computation.3 | async-start | bytes 2359296 | tf_op jit(solution)/shard_map/all_gather | solution.py:423
  18.9 1398.6 %all-reduce.19.cloned.1.call-start = ((), (), s32[]{:S(2)}) async-start(), calls=%async_computation.4 | async-start | bytes 12099584
  25.0 162.0 %copy-start.158 = (f32[1,512]{1,0:T(1,128)}, f32[1,512]{1,0:T(1,128)S(1)}, u32[]{:S(2)}) copy-start(f32[1,512]{1,0:T(1,128)S(1)} %get-tuple-element.242) | copy-start | bytes 6148
  25.0 166.5 %copy-start.231 = (f32[1,512]{1,0:T(1,128)}, f32[1,512]{1,0:T(1,128)S(1)}, u32[]{:S(2)}) copy-start(f32[1,512]{1,0:T(1,128)S(1)} %get-tuple-element.241) | copy-start | bytes 6148
  25.9 44.8 %copy-start.240 = (f32[256]{0:T(256)}, f32[256]{0:T(256)S(1)}, u32[]{:S(2)}) copy-start(f32[256]{0:T(256)S(1)} %get-tuple-element.289) | copy-start | bytes 3076
  25.9 47.2 %copy-start.244 = (f32[256]{0:T(256)}, f32[256]{0:T(256)S(1)}, u32[]{:S(2)}) copy-start(f32[256]{0:T(256)S(1)} %get-tuple-element.290) | copy-start | bytes 3076
  26.3 46.8 %copy-start.255 = (f32[256]{0:T(256)}, f32[256]{0:T(256)S(1)}, u32[]{:S(2)}) copy-start(f32[256]{0:T(256)S(1)} %add_rsqrt_fusion.11) | copy-start | bytes 3076
  73.1 59.1 %copy-start.94 = (f32[256,2048]{1,0:T(8,128)}, f32[256,2048]{1,0:T(8,128)S(1)}, u32[]{:S(2)}) copy-start(f32[256,2048]{1,0:T(8,128)S(1)} %fusion.14) | copy-start | bytes 6291460
  132.2 35.7 %copy-start.53 = (f32[256,512]{1,0:T(8,128)}, f32[256,512]{1,0:T(8,128)S(1)}, u32[]{:S(2)}) copy-start(f32[256,512]{1,0:T(8,128)S(1)} %get-tuple-element.270) | copy-start | bytes 1572868
  132.2 35.7 %copy-start.280 = (f32[256]{0:T(256)}, f32[256]{0:T(256)S(1)}, u32[]{:S(2)}) copy-start(f32[256]{0:T(256)S(1)} %broadcast_multiply_fusion.34) | copy-start | bytes 3076
  132.4 35.5 %copy-start.335 = (f32[256]{0:T(256)}, f32[256]{0:T(256)S(1)}, u32[]{:S(2)}) copy-start(f32[256]{0:T(256)S(1)} %add_rsqrt_fusion.10) | copy-start | bytes 3076
  168.1 27.6 %copy-start.51 = (bf16[1,256,512]{1,2,0:T(8,128)(2,1)}, bf16[1,256,512]{1,2,0:T(8,128)(2,1)S(1)}, u32[]{:S(2)}) copy-start(bf16[1,256,512]{1,2,0:T(8,128)(2,1)S(1)} %copy.203) | copy-start | bytes 786436
  194.0 183.4 %copy-start.50 = (bf16[1,256,512]{1,2,0:T(8,128)(2,1)}, bf16[1,256,512]{1,2,0:T(8,128)(2,1)S(1)}, u32[]{:S(2)}) copy-start(bf16[1,256,512]{1,2,0:T(8,128)(2,1)S(1)} %copy.211) | copy-start | bytes 786436
  246.7 36.1 %copy-start.23 = (f32[256,512]{1,0:T(8,128)}, f32[256,512]{1,0:T(8,128)S(1)}, u32[]{:S(2)}) copy-start(f32[256,512]{1,0:T(8,128)S(1)} %get-tuple-element.264) | copy-start | bytes 1572868
  246.8 36.1 %copy-start.238 = (f32[256]{0:T(256)}, f32[256]{0:T(256)S(1)}, u32[]{:S(2)}) copy-start(f32[256]{0:T(256)S(1)} %broadcast_multiply_fusion.27) | copy-start | bytes 3076
  247.0 35.8 %copy-start.253 = (f32[256]{0:T(256)}, f32[256]{0:T(256)S(1)}, u32[]{:S(2)}) copy-start(f32[256]{0:T(256)S(1)} %add_rsqrt_fusion.3) | copy-start | bytes 3076
  248.3 20.8 %copy-start.43 = (f32[256,512]{1,0:T(8,128)}, f32[256,512]{1,0:T(8,128)S(1)}, u32[]{:S(2)}) copy-start(f32[256,512]{1,0:T(8,128)S(1)} %slice_multiply_fusion.2) | copy-start | bytes 1572868
  251.0 18.1 %copy-start.66 = (f32[256,512]{1,0:T(8,128)}, f32[256,512]{1,0:T(8,128)S(1)}, u32[]{:S(2)}) copy-start(f32[256,512]{1,0:T(8,128)S(1)} %get-tuple-element.185) | copy-start | bytes 1572868
  251.0 18.1 %copy-start.278 = (f32[256]{0:T(256)}, f32[256]{0:T(256)S(1)}, u32[]{:S(2)}) copy-start(f32[256]{0:T(256)S(1)} %broadcast_multiply_fusion.26) | copy-start | bytes 3076
  251.3 17.8 %copy-start.329 = (f32[256]{0:T(256)}, f32[256]{0:T(256)S(1)}, u32[]{:S(2)}) copy-start(f32[256]{0:T(256)S(1)} %add_rsqrt_fusion.2) | copy-start | bytes 3076
  251.8 13.7 copy-start.222
  265.5 15.4 %copy-start.146 = (f32[256,512]{1,0:T(8,128)}, f32[256,512]{1,0:T(8,128)S(1)}, u32[]{:S(2)}) copy-start(f32[256,512]{1,0:T(8,128)S(1)} %get-tuple-element.200) | copy-start | bytes 1572868
  266.6 16.2 %copy-start.108 = (f32[256,512]{1,0:T(8,128)}, f32[256,512]{1,0:T(8,128)S(1)}, u32[]{:S(2)}) copy-start(f32[256,512]{1,0:T(8,128)S(1)} %get-tuple-element.202) | copy-start | bytes 1572868
  438.5 16.5 %copy-start.126 = (bf16[512,256]{0,1:T(8,128)(2,1)S(1)}, bf16[512,256]{0,1:T(8,128)(2,1)}, u32[]{:S(2)}) copy-start(bf16[512,256]{0,1:T(8,128)(2,1)} %get-tuple-element.198) | copy-start | bytes 786436
  438.5 16.7 %copy-start.142 = (bf16[256,2048]{1,0:T(8,128)(2,1)S(1)}, bf16[256,2048]{1,0:T(8,128)(2,1)}, u32[]{:S(2)}) copy-start(bf16[256,2048]{1,0:T(8,128)(2,1)} %copy-done.141) | copy-start | bytes 3145732
  1272.4 14.4 copy-start.237
  1450.5 13.7 copy-start.72
  1471.5 12.9 copy-start.347
  1485.3 13.4 copy-start.15
  (330 other events, 1066.4 us)
Sparse Core Ops, SparseCore 0:
  11.2 59.4 all-gather.4
  72.8 56.9 all-gather.6
  131.9 33.0 all-gather.8
  167.0 27.2 all-gather.10
  1283.4 134.1 all-reduce.18
where the time goes:
time: 1540 us; the launch traced here: 1520 us
  local copies, waits for them, and re-layouts  617 us (40%)
  blocking collectives  403 us (26%)
  waiting for transfers between devices  252 us (16%)
  other arithmetic  132 us (9%)
  matrix products  92 us (6%)
  between operations  20.2 us (1%)
    unnamed x755, local copies, waits for them, and re-layouts  426 us
    unnamed x1, blocking collectives  392 us
    unnamed x6, waiting for transfers between devices  124 us
    reshape x2, local copies, waits for them, and re-layouts, body(): lined.reshape(shards, groups, owned_count // groups)  64.1 us
    all_gather x1, waiting for transfers between devices, body(): lax.all_gather(ffn_out.astype(jnp.bfloat16), 'shard', axis=1, tiled=True)  56.7 us
    all_gather x1, waiting for transfers between devices, body(): lax.all_gather(ffn_in.astype(jnp.bfloat16), 'shard', axis=1, tiled=True)  39 us
    all_gather x1, waiting for transfers between devices, body(): lax.all_gather(attn_proj.astype(jnp.bfloat16), 'shard', axis=1, tiled=True)  32.6 us
  transfers between devices with their start and end apart: 5, of which 4 were waited for; matrix products, arithmetic and copies ran while one was open for 4% of the time, Pallas kernels for 0%

commit v1 on v0

v1 whole, which is shorter than its diff:
```python
import math

import jax
import jax.numpy as jnp
from jax import lax
from jax.experimental import pallas as pl
from jax.experimental.pallas import tpu as pltpu
from jax.sharding import PartitionSpec as P

D = 512
FF = 2048
HEADS = 8
HEAD = 64
KERNEL = 31
BACK = 64
AHEAD = 8
RELS = 73
STEP = 10
PIECES = 32
LEAD = 32
FFN_ROWS = 128
ATTN_ROWS = 64
CONV_ROWS = 48

NORM_EPSILON = 1e-05
ADAM_EPSILON = 1e-06
RATIO_EPSILON = 1e-06
BETA_FIRST = 0.9
BETA_SECOND = 0.999
WEIGHT_DECAY = 0.01
LEARN_RATE = 0.5
MASKED_SCORE = -1e30

bf16 = jnp.bfloat16
f32 = jnp.float32
VMEM_LIMIT = 60 * 1024 * 1024


def vmem():
    return pl.BlockSpec(memory_space=pltpu.VMEM)


def smem():
    return pl.BlockSpec(memory_space=pltpu.SMEM)


def shape(dims, kind):
    return jax.ShapeDtypeStruct(dims, kind)


def dot(left, right):
    return jnp.dot(left, right, preferred_element_type=f32)


def dot_rows(left, right):
    return lax.dot_general(left, right, (((0,), (0,)), ((), ())), preferred_element_type=f32)


def dot_cols(left, right):
    return lax.dot_general(left, right, (((1,), (1,)), ((), ())), preferred_element_type=f32)


def stats(values):
    centred = values - jnp.mean(values, axis=-1, keepdims=True)
    scale = lax.rsqrt(jnp.mean(centred * centred, axis=-1, keepdims=True) + NORM_EPSILON)
    return centred * scale, scale


def norm_back(grad, normed, scale, gain):
    grad_gain = jnp.sum(grad * normed, axis=0, keepdims=True)
    scaled = grad * gain
    inner = jnp.mean(scaled * normed, axis=-1, keepdims=True)
    back = scale * (scaled - jnp.mean(scaled, axis=-1, keepdims=True) - normed * inner)
    return back, grad_gain


def logistic(values):
    return 1.0 / (1.0 + jnp.exp(-values))


def slope_of(values, sig):
    return sig * (1.0 + values * (1.0 - sig))


class Plan:
    def __init__(self, groups, shards):
        self.groups, self.shards = groups, shards
        shard_bits = shards.bit_length() - 1
        group_bits = groups.bit_length() - 1
        self.used = min(5 - shard_bits, group_bits)
        self.owned = PIECES // shards
        order = [("group", 0)] + [("shard", b) for b in range(shard_bits)]
        order += [("group", b) for b in range(1, self.used)]
        self.order = order
        self.rest = [("group", b) for b in range(self.used, group_bits)]
        self.shard_bits = [("shard", b) for b in range(shard_bits)]
        self.kept = [step for step in order if step[0] == "group"]

    def piece_bit(self, step):
        return step[1] if step[0] == "group" else self.used + step[1]

    def place(self, piece):
        out = 0
        for step in self.order:
            out = out * 2 + ((piece >> self.piece_bit(step)) & 1)
        return out

    def kept_place(self, piece):
        out = 0
        for step in self.kept:
            out = out * 2 + ((piece >> step[1]) & 1)
        return out


def swap(values, step):
    axis, bit = step
    count = lax.axis_size(axis)
    return lax.ppermute(values, axis, [(i, i ^ (1 << bit)) for i in range(count)])


def add_low(left, right):
    return (left.astype(f32) + right.astype(f32)).astype(bf16)


def sum_pieces(pieces, plan):
    for step in plan.order:
        half = pieces.shape[0] // 2
        pieces = add_low(pieces[:half], swap(pieces[half:], step))
    for step in plan.rest:
        pieces = add_low(pieces, swap(pieces, step))
    for step in reversed(plan.kept):
        pieces = jnp.concatenate([pieces, swap(pieces, step)], axis=0)
    return pieces


def sum_everywhere(values, plan):
    for step in plan.order + plan.rest:
        values = values + swap(values, step)
    return values


def sum_shards(values, plan):
    for step in plan.shard_bits:
        values = values + swap(values, step)
    return values


def fetch(own, dim, plan, core):
    low = own.astype(bf16)
    if plan.shards != 2:
        return (lax.all_gather(low, "shard", axis=dim, tiled=True),)
    half = own.shape[dim] // 2
    mine = lax.dynamic_slice_in_dim(own, core * half, half, axis=dim).astype(bf16)
    near = swap(mine, ("shard", 0))
    far = swap(near, ("group", 0))
    return (low, near, far)


def join(place_ref, part_refs, whole_ref):
    if len(part_refs) == 1:
        whole_ref[...] = part_refs[0][...]
        return
    own, near, far = part_refs
    rows = own.shape[-2]
    half = rows // 2
    shard, core = place_ref[0], place_ref[1]
    first = pl.multiple_of(shard * rows, half)
    second = pl.multiple_of((1 - shard) * rows + core * half, half)
    third = pl.multiple_of((1 - shard) * rows + (1 - core) * half, half)
    if len(own.shape) == 2:
        whole_ref[pl.ds(first, rows), :] = own[...]
        whole_ref[pl.ds(second, half), :] = near[...]
        whole_ref[pl.ds(third, half), :] = far[...]
    else:
        for k in range(own.shape[0]):
            whole_ref[k, pl.ds(first, rows), :] = own[k]
            whole_ref[k, pl.ds(second, half), :] = near[k]
            whole_ref[k, pl.ds(third, half), :] = far[k]


def put(out_ref, plan, mine, value, row, rows_each, first):
    low = value.astype(bf16)
    for k in range(value.shape[0] // rows_each):
        spot = jnp.bitwise_xor(jnp.int32(plan.place(first + k)), mine)
        out_ref[spot, row : row + rows_each, :] = low[k * rows_each : (k + 1) * rows_each]


def call(kernel, outs, ins, specs=None, scratch=(), name=None, flops=0, nbytes=0, aliases=None):
    if specs is None:
        specs = [vmem()] * len(ins)
    cost = pl.CostEstimate(flops=int(flops), transcendentals=0, bytes_accessed=int(nbytes))
    return pl.pallas_call(
        kernel,
        out_shape=outs,
        in_specs=specs,
        out_specs=[vmem() for _ in outs],
        scratch_shapes=list(scratch),
        compiler_params=pltpu.CompilerParams(vmem_limit_bytes=VMEM_LIMIT),
        cost_estimate=cost,
        name=name,
    )(*ins)


def ffn_ahead(values, gain, win, wout, entry_ref, hidden_ref, slope_ref):
    normed, _ = stats(values)
    entry = (normed * gain).astype(bf16)
    entry_ref[...] = entry
    total = jnp.zeros(values.shape, f32)
    for b in range(FF // D):
        cols = slice(b * D, (b + 1) * D)
        before = dot(entry, win[:, cols])
        sig = logistic(before)
        hidden = (before * sig).astype(bf16)
        hidden_ref[:, cols] = hidden
        slope_ref[:, cols] = slope_of(before, sig).astype(bf16)
        total = total + dot(hidden, wout[cols, :])
    return total


def ffn_behind(grad, values, gain, win, wout, entry_ref, hidden_ref, slope_ref, out_ref, plan, mine):
    normed, scale = stats(values)
    entry = entry_ref[...]
    branch = (0.5 * grad).astype(bf16)
    grad_entry = jnp.zeros(values.shape, f32)
    for b in range(FF // D):
        cols = slice(b * D, (b + 1) * D)
        put(out_ref, plan, mine, dot_rows(hidden_ref[:, cols], branch), 64, 64, 8 * b)
        grad_before = (dot_cols(branch, wout[cols, :]) * slope_ref[:, cols].astype(f32)).astype(bf16)
        put(out_ref, plan, mine, dot_rows(entry, grad_before), 16 * b, 16, 0)
        grad_entry = grad_entry + dot_cols(grad_before, win[:, cols])
    back, grad_gain = norm_back(grad_entry, normed, scale, gain)
    return grad + back, grad_gain


def ffn_first(frames, vec, win_parts, wout_parts, place, plan):
    rows = frames.shape[0]
    n = len(win_parts)

    def kernel(place_ref, x_ref, vec_ref, *rest):
        wins, wouts = rest[:n], rest[n : 2 * n]
        out_ref, entry_ref, hidden_ref, slope_ref, win, wout = rest[2 * n :]
        join(place_ref, wins, win)
        join(place_ref, wouts, wout)
        values = x_ref[...].astype(f32)
        total = ffn_ahead(values, vec_ref[31:32, :], win, wout, entry_ref, hidden_ref, slope_ref)
        out_ref[...] = values + 0.5 * total

    return call(
        kernel,
        [shape((rows, D), f32), shape((rows, D), bf16), shape((rows, FF), bf16), shape((rows, FF), bf16)],
        [place, frames, vec, *win_parts, *wout_parts],
        [smem()] + [vmem()] * (2 + 2 * n),
        [pltpu.VMEM((D, FF), bf16), pltpu.VMEM((FF, D), bf16)],
        "ffn_first",
        4 * rows * D * FF,
        12e6,
    )


def ffn_last(values, vec, cotangent, lengths, win_parts, wout_parts, place, plan):
    rows = values.shape[0]
    count = lengths.shape[0]
    n = len(win_parts)

    def kernel(place_ref, len_ref, x_ref, vec_ref, cot_ref, *rest):
        wins, wouts = rest[:n], rest[n : 2 * n]
        y_ref, dx_ref, gain_ref, g_ref, win, wout, entry_ref, hidden_ref, slope_ref = rest[2 * n :]
        join(place_ref, wins, win)
        join(place_ref, wouts, wout)
        x = x_ref[...]
        gain = vec_ref[35:36, :]
        total = ffn_ahead(x, gain, win, wout, entry_ref, hidden_ref, slope_ref)
        normed, scale = stats(x + 0.5 * total)
        top = vec_ref[36:37, :]
        y_ref[...] = (normed * top).astype(bf16)
        each = rows // count
        grads = []
        for s in range(count):
            spot = lax.broadcasted_iota(jnp.int32, (each, 1), 0)
            part = cot_ref[s * each : (s + 1) * each, :].astype(f32)
            grads.append(jnp.where(spot < len_ref[s], part, 0.0))
        back, grad_top = norm_back(jnp.concatenate(grads, axis=0), normed, scale, top)
        grad, grad_gain = ffn_behind(
            back, x, gain, win, wout, entry_ref, hidden_ref, slope_ref, g_ref, plan, place_ref[2]
        )
        dx_ref[...] = grad
        gain_ref[...] = jnp.concatenate([grad_gain, grad_top, jnp.zeros((6, D), f32)], axis=0)

    return call(
        kernel,
        [shape((rows, D), bf16), shape((rows, D), f32), shape((8, D), f32), shape((PIECES, FFN_ROWS, D), bf16)],
        [place, lengths, values, vec, cotangent, *win_parts, *wout_parts],
        [smem(), smem()] + [vmem()] * (3 + 2 * n),
        [
            pltpu.VMEM((D, FF), bf16),
            pltpu.VMEM((FF, D), bf16),
            pltpu.VMEM((rows, D), bf16),
            pltpu.VMEM((rows, FF), bf16),
            pltpu.VMEM((rows, FF), bf16),
        ],
        "ffn_last",
        12 * rows * D * FF,
        16e6,
    )


def ffn_first_back(grad, frames, vec, kept, win_parts, wout_parts, place, plan):
    rows = frames.shape[0]
    n = len(win_parts)
    entry, hidden, slope = kept

    def kernel(place_ref, grad_ref, x_ref, vec_ref, entry_ref, hidden_ref, slope_ref, *rest):
        wins, wouts = rest[:n], rest[n : 2 * n]
        dx_ref, gain_ref, g_ref, win, wout = rest[2 * n :]
        join(place_ref, wins, win)
        join(place_ref, wouts, wout)
        back, grad_gain = ffn_behind(
            grad_ref[...],
            x_ref[...].astype(f32),
            vec_ref[31:32, :],
            win,
            wout,
            entry_ref,
            hidden_ref,
            slope_ref,
            g_ref,
            plan,
            place_ref[2],
        )
        dx_ref[...] = back.astype(bf16)
        gain_ref[...] = jnp.concatenate([grad_gain, jnp.zeros((7, D), f32)], axis=0)

    return call(
        kernel,
        [shape((rows, D), bf16), shape((8, D), f32), shape((PIECES, FFN_ROWS, D), bf16)],
        [place, grad, frames, vec, entry, hidden, slope, *win_parts, *wout_parts],
        [smem()] + [vmem()] * (6 + 2 * n),
        [pltpu.VMEM((D, FF), bf16), pltpu.VMEM((FF, D), bf16)],
        "ffn_first_back",
        8 * rows * D * FF,
        16e6,
    )


def attend(values, vec, rel_table, lengths, parts, place, plan):
    rows = values.shape[0]
    count = lengths.shape[0]
    each = rows // count
    n = len(parts)
    pairs = HEADS // 2

    def kernel(place_ref, len_ref, x_ref, vec_ref, rel_ref, *rest):
        ws = rest[:n]
        out_ref, entry_ref, qkv_ref, prob_ref, mix_ref, weight, mixed = rest[n:]
        join(place_ref, ws, weight)
        x = x_ref[...]
        normed, _ = stats(x)
        entry = (normed * vec_ref[32:33, :]).astype(bf16)
        entry_ref[...] = entry
        for k in range(3):
            heads = dot(entry, weight[k]).astype(bf16)
            for p in range(pairs):
                qkv_ref[k, p] = heads[:, p * 128 : (p + 1) * 128]
        lane = lax.broadcasted_iota(jnp.int32, (1, 128), 1)
        table = rel_ref[...]
        spot = lax.broadcasted_iota(jnp.int32, (1, each), 1)

        def step(i, carry):
            s = i // pairs
            p = i % pairs
            span = pl.ds(pl.multiple_of(s * each, each), each)
            query = qkv_ref[0, p, span, :]
            keys = qkv_ref[1, p, span, :]
            vals = qkv_ref[2, p, span, :]
            valid = spot < len_ref[s]
            both = []
            for h in range(2):
                mask = (lane < HEAD) if h == 0 else (lane >= HEAD)
                mine = jnp.where(mask, query, jnp.zeros_like(query))
                raw = dot_cols(mine, keys)
                skew = pltpu.roll(dot_cols(mine, table), 0, 1, stride=1, stride_axis=0)[:, :each]
                scores = jnp.where(valid, (raw + skew) * 0.125, MASKED_SCORE)
                grown = jnp.exp(scores - jnp.max(scores, axis=-1, keepdims=True))
                low = (grown * (1.0 / jnp.sum(grown, axis=-1, keepdims=True))).astype(bf16)
                prob_ref[2 * i + h] = low
                both.append(dot(low, vals))
            mixed[p, span, :] = jnp.where(lane < HEAD, both[0], both[1]).astype(bf16)
            return carry

        lax.fori_loop(0, count * pairs, step, 0)
        mix = jnp.concatenate([mixed[p] for p in range(pairs)], axis=1)
        mix_ref[...] = mix
        out_ref[...] = x + dot(mix, weight[3])

    return call(
        kernel,
        [
            shape((rows, D), f32),
            shape((rows, D), bf16),
            shape((3, pairs, rows, 128), bf16),
            shape((count * HEADS, each, each), bf16),
            shape((rows, D), bf16),
        ],
        [place, lengths, values, vec, rel_table, *parts],
        [smem(), smem()] + [vmem()] * (3 + n),
        [pltpu.VMEM((4, D, D), bf16), pltpu.VMEM((pairs, rows, 128), bf16)],
        "attend",
        16 * rows * D * D,
        20e6,
    )


def attend_back(grad, values, vec, kept, rel_table, parts, place, plan, count):
    rows = values.shape[0]
    each = rows // count
    n = len(parts)
    pairs = HEADS // 2
    entry, qkv, prob, mix = kept
    width = rel_table.shape[0]

    def kernel(place_ref, grad_ref, x_ref, vec_ref, entry_ref, qkv_ref, prob_ref, mix_ref, rel_ref, *rest):
        ws = rest[:n]
        dx_ref, gain_ref, rel_out, g_ref, weight, dmix, dqkv = rest[n:]
        mine_spot = place_ref[2]
        join(place_ref, ws, weight)
        down = grad_ref[...]
        low = down.astype(bf16)
        put(g_ref, plan, mine_spot, dot_rows(mix_ref[...], low), 48, 16, 0)
        spread = dot_cols(low, weight[3]).astype(bf16)
        for p in range(pairs):
            dmix[p] = spread[:, p * 128 : (p + 1) * 128]
        lane = lax.broadcasted_iota(jnp.int32, (1, 128), 1)
        table = rel_ref[...]
        flip = (
            lax.broadcasted_iota(jnp.int32, (each, each), 0)
            + lax.broadcasted_iota(jnp.int32, (each, each), 1)
            == each - 1
        ).astype(bf16)
        rel_out[...] = jnp.zeros_like(rel_out)

        def step(i, carry):
            s = i // pairs
            p = i % pairs
            span = pl.ds(pl.multiple_of(s * each, each), each)
            query = qkv_ref[0, p, span, :]
            keys = qkv_ref[1, p, span, :]
            vals = qkv_ref[2, p, span, :]
            outer = dmix[p, span, :]
            grad_q = jnp.zeros((each, 128), f32)
            grad_k = jnp.zeros((each, 128), f32)
            grad_v = jnp.zeros((each, 128), f32)
            grad_r = jnp.zeros((width, 128), f32)
            for h in range(2):
                mask = (lane < HEAD) if h == 0 else (lane >= HEAD)

                def pick(v):
                    return jnp.where(mask, v, jnp.zeros_like(v))

                dout = pick(outer)
                q_own = pick(query)
                prob_low = prob_ref[2 * i + h]
                prob_wide = prob_low.astype(f32)
                dprob = dot_cols(dout, vals)
                inner = jnp.sum(prob_wide * dprob, axis=-1, keepdims=True)
                dscore = (prob_wide * (dprob - inner)).astype(bf16)
                grad_v = grad_v + dot_rows(prob_low, dout)
                grad_k = grad_k + dot_rows(dscore, q_own)
                turned = dot(flip, dscore)
                wide = jnp.concatenate([turned, jnp.zeros((each, width - each), f32)], axis=1)
                skew = pltpu.roll(wide, width - each + 1, 1, stride=1, stride_axis=0).astype(bf16)
                along = dot(flip, skew).astype(bf16)
                grad_q = grad_q + dot(dscore, pick(keys)) + dot(along, pick(table))
                grad_r = grad_r + dot_rows(along, q_own)
            dqkv[0, p, span, :] = (grad_q * 0.125).astype(bf16)
            dqkv[1, p, span, :] = (grad_k * 0.125).astype(bf16)
            dqkv[2, p, span, :] = grad_v.astype(bf16)
            rel_out[...] += grad_r * 0.125
            return carry

        lax.fori_loop(0, count * pairs, step, 0)
        entry_low = entry_ref[...]
        grad_entry = jnp.zeros((rows, D), f32)
        for k in range(3):
            heads = jnp.concatenate([dqkv[k, p] for p in range(pairs)], axis=1)
            put(g_ref, plan, mine_spot, dot_rows(entry_low, heads), 16 * k, 16, 0)
            grad_entry = grad_entry + dot_cols(heads, weight[k])
        normed, scale = stats(x_ref[...])
        back, grad_gain = norm_back(grad_entry, normed, scale, vec_ref[32:33, :])
        dx_ref[...] = down + back
        gain_ref[...] = jnp.concatenate([grad_gain, jnp.zeros((7, D), f32)], axis=0)

    return call(
        kernel,
        [
            shape((rows, D), f32),
            shape((8, D), f32),
            shape((width, 128), f32),
            shape((PIECES, ATTN_ROWS, D), bf16),
        ],
        [place, grad, values, vec, entry, qkv, prob, mix, rel_table, *parts],
        [smem()] + [vmem()] * (8 + n),
        [
            pltpu.VMEM((4, D, D), bf16),
            pltpu.VMEM((pairs, rows, 128), bf16),
            pltpu.VMEM((3, pairs, rows, 128), bf16),
        ],
        "attend_back",
        50 * rows * D * D,
        24e6,
    )


def convolve(values, vec, parts, place, plan, count):
    rows = values.shape[0]
    each = rows // count
    n = len(parts)
    cols = D // 128
    chunk = 64

    def kernel(place_ref, x_ref, vec_ref, *rest):
        ws = rest[:n]
        out_ref, entry_ref, gated_ref, sig_ref, conv_ref, act_ref, weight = rest[n:]
        join(place_ref, ws, weight)
        x = x_ref[...]
        normed, _ = stats(x)
        entry = (normed * vec_ref[33:34, :]).astype(bf16)
        entry_ref[...] = entry
        linear = dot(entry, weight[:, :D])
        sig = logistic(dot(entry, weight[:, D : 2 * D]))
        sig_ref[...] = sig
        gated = linear * sig
        for s in range(count):
            for c in range(cols):
                gated_ref[s, c, :LEAD, :] = jnp.zeros((LEAD, 128), f32)
                gated_ref[s, c, LEAD:, :] = gated[s * each : (s + 1) * each, c * 128 : (c + 1) * 128]
        for c in range(cols):
            taps = vec_ref[0:32, c * 128 : (c + 1) * 128]

            def step(i, carry):
                s = i // (each // chunk)
                t = (i % (each // chunk)) * chunk
                total = jnp.zeros((chunk, 128), f32)
                for k in range(KERNEL):
                    total = total + taps[k : k + 1] * gated_ref[s, c, pl.ds(t + k + LEAD - KERNEL + 1, chunk), :]
                conv_ref[pl.ds(pl.multiple_of(i * chunk, chunk), chunk), c * 128 : (c + 1) * 128] = total
                return carry

            lax.fori_loop(0, rows // chunk, step, 0)
        inner, _ = stats(conv_ref[...])
        act = inner * vec_ref[34:35, :]
        low = (act * logistic(act)).astype(bf16)
        act_ref[...] = low
        out_ref[...] = x + dot(low, weight[:, 2 * D :])

    return call(
        kernel,
        [
            shape((rows, D), f32),
            shape((rows, D), bf16),
            shape((count, cols, each + LEAD, 128), f32),
            shape((rows, D), f32),
            shape((rows, D), f32),
            shape((rows, D), bf16),
        ],
        [place, values, vec, *parts],
        [smem()] + [vmem()] * (2 + n),
        [pltpu.VMEM((D, 3 * D), bf16)],
        "convolve",
        12 * rows * D * D,
        16e6,
    )


def convolve_back(grad, values, vec, kept, parts, place, plan, count):
    rows = values.shape[0]
    each = rows // count
    n = len(parts)
    cols = D // 128
    entry, gated, sig, conved, act = kept

    def kernel(place_ref, grad_ref, x_ref, vec_ref, entry_ref, gated_ref, sig_ref, conv_ref, act_ref, *rest):
        ws = rest[:n]
        dx_ref, gain_ref, taps_out, g_ref, weight, dconv, dgated = rest[n:]
        mine = place_ref[1 + 1]
        join(place_ref, ws, weight)
        down = grad_ref[...]
        low = down.astype(bf16)
        put(g_ref, plan, mine, dot_rows(act_ref[...], low), 32, 16, 0)
        inner, inner_scale = stats(conv_ref[...])
        inner_gain = vec_ref[34:35, :]
        act_in = inner * inner_gain
        grad_act = dot_cols(low, weight[:, 2 * D :]) * slope_of(act_in, logistic(act_in))
        grad_conv, gain_inner = norm_back(grad_act, inner, inner_scale, inner_gain)
        for s in range(count):
            for c in range(cols):
                dconv[s, c, :each, :] = grad_conv[s * each : (s + 1) * each, c * 128 : (c + 1) * 128]
                dconv[s, c, each:, :] = jnp.zeros((LEAD, 128), f32)
        for c in range(cols):
            lanes = slice(c * 128, (c + 1) * 128)
            taps = vec_ref[0:32, lanes]

            def step(i, sums):
                s = i // (each // 8)
                t = (i % (each // 8)) * 8
                here = dconv[s, c, pl.ds(pl.multiple_of(t, 8), 8), :]
                total = jnp.zeros((8, 128), f32)
                new = []
                for k in range(KERNEL):
                    new.append(sums[k] + here * gated_ref[s, c, pl.ds(t + k + LEAD - KERNEL + 1, 8), :])
                    total = total + taps[k : k + 1] * dconv[s, c, pl.ds(t + KERNEL - 1 - k, 8), :]
                dgated[pl.ds(pl.multiple_of(i * 8, 8), 8), lanes] = total
                return tuple(new)

            sums = lax.fori_loop(0, rows // 8, step, tuple(jnp.zeros((8, 128), f32) for _ in range(KERNEL)))
            found = [jnp.sum(v, axis=0, keepdims=True) for v in sums]
            taps_out[:, lanes] = jnp.concatenate(found + [jnp.zeros((1, 128), f32)], axis=0)
        grad_gated = dgated[...]
        sig_wide = sig_ref[...]
        linear_sig = jnp.concatenate(
            [
                jnp.concatenate([gated_ref[s, c, LEAD:, :] for c in range(cols)], axis=1)
                for s in range(count)
            ],
            axis=0,
        )
        grad_one = (grad_gated * sig_wide).astype(bf16)
        grad_two = (grad_gated * linear_sig * (1.0 - sig_wide)).astype(bf16)
        entry_low = entry_ref[...]
        put(g_ref, plan, mine, dot_rows(entry_low, grad_one), 0, 16, 0)
        put(g_ref, plan, mine, dot_rows(entry_low, grad_two), 16, 16, 0)
        grad_entry = dot_cols(grad_one, weight[:, :D]) + dot_cols(grad_two, weight[:, D : 2 * D])
        normed, scale = stats(x_ref[...])
        back, gain_outer = norm_back(grad_entry, normed, scale, vec_ref[33:34, :])
        dx_ref[...] = down + back
        gain_ref[...] = jnp.concatenate([gain_outer, gain_inner, jnp.zeros((6, D), f32)], axis=0)

    return call(
        kernel,
        [
            shape((rows, D), f32),
            shape((8, D), f32),
            shape((32, D), f32),
            shape((PIECES, CONV_ROWS, D), bf16),
        ],
        [place, grad, values, vec, entry, gated, sig, conved, act, *parts],
        [smem()] + [vmem()] * (8 + n),
        [
            pltpu.VMEM((D, 3 * D), bf16),
            pltpu.VMEM((count, cols, each + LEAD, 128), f32),
            pltpu.VMEM((rows, D), f32),
        ],
        "convolve_back",
        40 * rows * D * D,
        20e6,
    )


def adam(weight, moment, square, grad):
    new_moment = BETA_FIRST * moment + (1.0 - BETA_FIRST) * grad
    new_square = BETA_SECOND * square + (1.0 - BETA_SECOND) * grad * grad
    first = new_moment * (1.0 / (1.0 - BETA_FIRST**STEP))
    second = new_square * (1.0 / (1.0 - BETA_SECOND**STEP))
    update = first / (jnp.sqrt(second) + ADAM_EPSILON) + WEIGHT_DECAY * weight
    return new_moment, new_square, update


def folded(values):
    squares = jnp.sum((values * values).reshape(-1, values.shape[-1]), axis=0, keepdims=True)
    total = squares[:, :128]
    for c in range(1, values.shape[-1] // 128):
        total = total + squares[:, c * 128 : (c + 1) * 128]
    return total


def update_ffn(layer, pieces, spots, states, given):
    count = pieces.shape[0]
    win, wout = states[0], states[3]
    in_rows, out_rows = win.shape[1] // count, wout.shape[1] // count
    outs = [win.shape] * 4 + [wout.shape] * 4
    if given is None:
        given = ()

    def kernel(spot_ref, g_ref, w0, m0, q0, w1, m1, q1, *rest):
        g0_out, u0_out, m0_out, q0_out, g1_out, u1_out, m1_out, q1_out, sums = rest[len(given) :]
        index = pl.program_id(0)

        @pl.when(index == 0)
        def _():
            sums[...] = jnp.zeros_like(sums)

        raw = g_ref[0].astype(f32)
        rows = []
        wide = jnp.concatenate([raw[k * 16 : k * 16 + 16] for k in range(FF // D)], axis=1)
        for weight, moment, square, grad, g_out, u_out, m_out, q_out in (
            (w0[0], m0[0], q0[0], wide, g0_out, u0_out, m0_out, q0_out),
            (w1[0], m1[0], q1[0], raw[64:128], g1_out, u1_out, m1_out, q1_out),
        ):
            new_moment, new_square, update = adam(weight, moment, square, grad)
            g_out[0] = grad
            u_out[0] = update
            m_out[0] = new_moment
            q_out[0] = new_square
            rows += [folded(weight), folded(update)]
        sums[...] += jnp.concatenate(rows + [jnp.zeros((4, 128), f32)], axis=0)

    def at_in(p, spot):
        return (layer, p, 0)

    in_block = pl.BlockSpec((1, in_rows, FF), at_in)
    out_block = pl.BlockSpec((1, out_rows, D), at_in)
    return pl.pallas_call(
        kernel,
        out_shape=[shape(dims, f32) for dims in outs] + [shape((8, 128), f32)],
        grid_spec=pltpu.PrefetchScalarGridSpec(
            num_scalar_prefetch=1,
            grid=(count,),
            in_specs=[pl.BlockSpec((1, FFN_ROWS, D), lambda p, spot: (spot[p], 0, 0))]
            + [in_block] * 3
            + [out_block] * 3
            + [pl.BlockSpec(memory_space=pl.ANY)] * len(given),
            out_specs=[in_block] * 4 + [out_block] * 4 + [pl.BlockSpec((8, 128), lambda p, spot: (0, 0))],
        ),
        input_output_aliases={8 + k: k for k in range(len(given))},
        compiler_params=pltpu.CompilerParams(vmem_limit_bytes=VMEM_LIMIT),
        cost_estimate=pl.CostEstimate(flops=0, transcendentals=0, bytes_accessed=32000000),
        name="update_ffn",
    )(spots, pieces, *states, *given)


def update_rest(attn_pieces, conv_pieces, spots, attn, conv):
    count = attn_pieces.shape[0]
    rows = attn[0].shape[1] // count

    def kernel(spot_ref, ga_ref, gc_ref, wa, ma, qa, wc, mc, qc, *outs):
        ga_out, ua_out, ma_out, qa_out, qo_out, gc_out, uc_out, mc_out, qc_out, sums = outs
        index = pl.program_id(0)

        @pl.when(index == 0)
        def _():
            sums[...] = jnp.zeros_like(sums)

        found = []
        for k in range(4):
            grad = ga_ref[0, k * 16 : (k + 1) * 16].astype(f32)
            weight = wa[k]
            new_moment, new_square, update = adam(weight, ma[k], qa[k], grad)
            ga_out[k] = grad
            ua_out[k] = update
            ma_out[k] = new_moment
            if k < 3:
                qa_out[k] = new_square
            else:
                qo_out[...] = new_square
            found += [folded(weight), folded(update)]
        for low, high in ((0, 2), (2, 3)):
            lanes = slice(low * D, high * D)
            grad = jnp.concatenate([gc_ref[0, k * 16 : (k + 1) * 16] for k in range(low, high)], axis=1)
            grad = grad.astype(f32)
            weight = wc[:, lanes]
            new_moment, new_square, update = adam(weight, mc[:, lanes], qc[:, lanes], grad)
            gc_out[:, lanes] = grad
            uc_out[:, lanes] = update
            mc_out[:, lanes] = new_moment
            qc_out[:, lanes] = new_square
            found += [folded(weight), folded(update)]
        sums[...] += jnp.concatenate(found + [jnp.zeros((4, 128), f32)], axis=0)

    attn_block = pl.BlockSpec((4, rows, D), lambda p, spot: (0, p, 0))
    conv_block = pl.BlockSpec((rows, 3 * D), lambda p, spot: (p, 0))
    three = pl.BlockSpec((3, rows, D), lambda p, spot: (0, p, 0))
    one = pl.BlockSpec((rows, D), lambda p, spot: (p, 0))
    side = attn[0].shape[1]
    return pl.pallas_call(
        kernel,
        out_shape=[shape(attn[0].shape, f32)] * 3
        + [shape((3, side, D), f32), shape((side, D), f32)]
        + [shape(conv[0].shape, f32)] * 4
        + [shape((16, 128), f32)],
        grid_spec=pltpu.PrefetchScalarGridSpec(
            num_scalar_prefetch=1,
            grid=(count,),
            in_specs=[
                pl.BlockSpec((1, ATTN_ROWS, D), lambda p, spot: (spot[p], 0, 0)),
                pl.BlockSpec((1, CONV_ROWS, D), lambda p, spot: (spot[p], 0, 0)),
            ]
            + [attn_block] * 3
            + [conv_block] * 3,
            out_specs=[attn_block] * 3
            + [three, one]
            + [conv_block] * 4
            + [pl.BlockSpec((16, 128), lambda p, spot: (0, 0))],
        ),
        compiler_params=pltpu.CompilerParams(vmem_limit_bytes=VMEM_LIMIT),
        cost_estimate=pl.CostEstimate(flops=0, transcendentals=0, bytes_accessed=28000000),
        name="update_rest",
    )(spots, attn_pieces, conv_pieces, *attn, *conv)


def move(weight, update, factor):
    return weight - LEARN_RATE * factor * update


def ratio_of(sums):
    weight, update = sums[0::2], sums[1::2]
    return jnp.sqrt(weight), jnp.sqrt(update), jnp.sqrt(weight) / jnp.sqrt(update + RATIO_EPSILON)


def body(
    frames,
    lengths,
    cotangent,
    ffn_in,
    ffn_in_moment,
    ffn_in_square,
    ffn_out,
    ffn_out_moment,
    ffn_out_square,
    attn_proj,
    attn_moment,
    attn_square,
    conv_proj,
    conv_moment,
    conv_square,
    vectors,
    vectors_moment,
    vectors_square,
    rel_keys,
    rel_moment,
    rel_square,
):
    groups, shards = lax.axis_size("group"), lax.axis_size("shard")
    plan = Plan(groups, shards)
    group, shard = lax.axis_index("group"), lax.axis_index("shard")
    core = jnp.bitwise_and(group, 1)
    count, each, _ = frames.shape
    mine = jnp.int32(0)
    for step in plan.order:
        bit = jnp.right_shift(group if step[0] == "group" else shard, step[1]) & 1
        mine = mine * 2 + bit
    kept = jnp.int32(0)
    for step in plan.kept:
        kept = kept * 2 + (jnp.right_shift(group, step[1]) & 1)
    spots = jnp.array([plan.kept_place(p) for p in range(plan.owned)], jnp.int32) ^ kept
    place = jnp.stack([shard, core, mine]).astype(jnp.int32)

    win0 = fetch(ffn_in[0], 0, plan, core)
    wout0 = fetch(ffn_out[0], 0, plan, core)
    vec = lax.all_gather(vectors.astype(bf16), "shard", axis=1, tiled=True) if shards != 2 else None
    if vec is None:
        low = vectors.astype(bf16)
        other = swap(low, ("shard", 0))
        vec = jnp.where(shard == 0, jnp.concatenate([low, other], 1), jnp.concatenate([other, low], 1))
    vec = jnp.concatenate([vec.astype(f32), jnp.zeros((3, D), f32)], axis=0)
    watt = fetch(attn_proj, 1, plan, core)
    wconv = fetch(conv_proj, 0, plan, core)
    win1 = fetch(ffn_in[1], 0, plan, core)
    wout1 = fetch(ffn_out[1], 0, plan, core)

    rel_low = rel_keys.astype(bf16)
    table = jnp.concatenate(
        [
            rel_low[BACK:],
            jnp.broadcast_to(rel_low[RELS - 1 :], (each - AHEAD - 1, HEAD)),
            jnp.broadcast_to(rel_low[:1], (each - BACK, HEAD)),
            rel_low[:BACK],
        ],
        axis=0,
    )
    table = jnp.concatenate([table, table], axis=1)

    flat = frames.reshape(count * each, D)
    x1, *kept_ffn = ffn_first(flat, vec, win0, wout0, place, plan)
    x2, *kept_attn = attend(x1, vec, table, lengths, watt, place, plan)
    x3, *kept_conv = convolve(x2, vec, wconv, place, plan, count)
    output, d3, gains_last, pieces_last = ffn_last(
        x3, vec, cotangent.reshape(count * each, D), lengths, win1, wout1, place, plan
    )
    owned_last = sum_pieces(pieces_last, plan)
    d2, gains_conv, taps, pieces_conv = convolve_back(d3, x2, vec, kept_conv, wconv, place, plan, count)
    owned_conv = sum_pieces(pieces_conv, plan)
    d1, gains_attn, rel_wide, pieces_attn = attend_back(d2, x1, vec, kept_attn, table, watt, place, plan, count)
    owned_attn = sum_pieces(pieces_attn, plan)
    d0, gains_first, pieces_first = ffn_first_back(d1, flat, vec, kept_ffn, win0, wout0, place, plan)
    owned_first = sum_pieces(pieces_first, plan)

    rel_half = rel_wide[:, :HEAD] + rel_wide[:, HEAD:]
    edge = 2 * each - BACK
    rel_local = jnp.concatenate(
        [
            jnp.sum(rel_half[each : edge + 1], axis=0, keepdims=True),
            rel_half[edge + 1 :],
            rel_half[:AHEAD],
            jnp.sum(rel_half[AHEAD:each], axis=0, keepdims=True),
        ],
        axis=0,
    )
    vec_local = jnp.concatenate(
        [taps[:KERNEL], gains_first[:1], gains_attn[:1], gains_conv[:2], gains_last[:2]], axis=0
    )
    rel_lines = jnp.pad(rel_local.reshape(-1), (0, 10 * D - RELS * HEAD)).reshape(10, D)
    small = sum_everywhere(jnp.concatenate([vec_local, rel_lines, jnp.zeros((1, D), f32)], axis=0), plan)
    wide = vectors.shape[1]
    vec_grad = lax.dynamic_slice(small, (0, shard * wide), (KERNEL + 6, wide))
    rel_grad = small[KERNEL + 6 : KERNEL + 16].reshape(-1)[: RELS * HEAD].reshape(RELS, HEAD)

    states = (ffn_in, ffn_in_moment, ffn_in_square, ffn_out, ffn_out_moment, ffn_out_square)
    *half_ffn, sums_last = update_ffn(1, owned_last, spots, states, None)
    (attn_grad, attn_up, attn_m, attn_q, attn_qo, conv_grad, conv_up, conv_m, conv_q, sums_rest) = update_rest(
        owned_attn,
        owned_conv,
        spots,
        (attn_proj, attn_moment, attn_square),
        (conv_proj, conv_moment, conv_square),
    )
    *full_ffn, sums_first = update_ffn(0, owned_first, spots, states, half_ffn)
    in_grad, in_up, in_m, in_q, out_grad, out_up, out_m, out_q = full_ffn
    vec_m, vec_q, vec_up = adam(vectors, vectors_moment, vectors_square, vec_grad)
    rel_m, rel_q, rel_up = adam(rel_keys, rel_moment, rel_square, rel_grad)

    vec_sums = []
    for part in (vectors, vec_up):
        squares = jnp.sum(part * part, axis=1)
        vec_sums.append(jnp.concatenate([jnp.sum(squares[:KERNEL])[None], squares[KERNEL:]]))
    early = sum_shards(jnp.sum(jnp.concatenate([sums_last, sums_rest], axis=0), axis=1), plan)
    late = sum_shards(
        jnp.concatenate([jnp.sum(sums_first[:4], axis=1), jnp.stack(vec_sums, axis=1).reshape(-1)]), plan
    )
    rel_sums = jnp.stack([jnp.sum(rel_keys * rel_keys), jnp.sum(rel_up * rel_up)])
    sums = jnp.concatenate(
        [
            jnp.stack([late[0], late[1], early[0], early[1], late[2], late[3], early[2], early[3]]),
            early[8:20],
            late[4:18],
            rel_sums,
        ]
    )
    weight_norms, update_norms, ratios = ratio_of(sums)
    conv_factor = jnp.where(jnp.arange(3 * D) < 2 * D, ratios[8], ratios[9])[None, :]
    vec_factor = jnp.concatenate([jnp.full((KERNEL,), ratios[10]), ratios[11:17]])[:, None]
    return (
        output.reshape(frames.shape),
        d0.reshape(frames.shape),
        in_grad,
        move(ffn_in, in_up, ratios[0:2][:, None, None]),
        in_m,
        in_q,
        out_grad,
        move(ffn_out, out_up, ratios[2:4][:, None, None]),
        out_m,
        out_q,
        attn_grad,
        move(attn_proj, attn_up, ratios[4:8][:, None, None]),
        attn_m,
        attn_q,
        attn_qo,
        conv_grad,
        move(conv_proj, conv_up, conv_factor),
        conv_m,
        conv_q,
        vec_grad,
        move(vectors, vec_up, vec_factor),
        vec_m,
        vec_q,
        rel_grad,
        move(rel_keys, rel_up, ratios[17]),
        rel_m,
        rel_q,
        jnp.stack([weight_norms, update_norms]),
    )


def solution(mesh):
    return jax.shard_map(
        body,
        mesh=mesh,
        in_specs=(
            P(("group", "shard"), None, None),
            P(("group", "shard")),
            P(("group", "shard"), None, None),
            P(None, "shard", None),
            P(None, "shard", None),
            P(None, "shard", None),
            P(None, "shard", None),
            P(None, "shard", None),
            P(None, "shard", None),
            P(None, "shard", None),
            P(None, "shard", None),
            P(None, "shard", None),
            P("shard", None),
            P("shard", None),
            P("shard", None),
            P(None, "shard"),
            P(None, "shard"),
            P(None, "shard"),
            P(),
            P(),
            P(),
        ),
        out_specs=(
            P(("group", "shard"), None, None),
            P(("group", "shard"), None, None),
            P(None, "shard", None),
            P(None, "shard", None),
            P(None, "shard", None),
            P(None, "shard", None),
            P(None, "shard", None),
            P(None, "shard", None),
            P(None, "shard", None),
            P(None, "shard", None),
            P(None, "shard", None),
            P(None, "shard", None),
            P(None, "shard", None),
            P(None, "shard", None),
            P("shard", None),
            P("shard", None),
            P("shard", None),
            P("shard", None),
            P("shard", None),
            P(None, "shard"),
            P(None, "shard"),
            P(None, "shard"),
            P(None, "shard"),
            P(),
            P(),
            P(),
            P(),
            P(),
        ),
        check_vma=False,
    )
```

time: 1540 us -> 466 us (0.30)
  local copies, waits for them, and re-layouts: 617 us -> 46 us
  blocking collectives: 403 us -> 0 us
  Pallas kernels: 0 us -> 153 us
  matrix products: 92 us -> 0 us
  waiting for transfers between devices: 252 us -> 161 us
  other arithmetic: 132 us -> 42.2 us
  starting transfers between devices: 0.21 us -> 52 us
  between operations: 20.2 us -> 2.6 us
    unnamed x755 -> x85, local copies, waits for them, and re-layouts: 426 us -> 12.4 us
    unnamed x1 -> x0, blocking collectives: 392 us -> none
    ppermute x0 -> x56, waiting for transfers between devices: none -> 161 us  [swap(): return lax.ppermute(values, axis, [(i, i ^ 1 << bit) for i in range(count)])]
    pallas_call x0 -> x10, Pallas kernels: none -> 153 us  [the longest x7 97.7 us: call(): pl.pallas_call(kernel, out_shape=outs, in_specs=specs, out_specs=[vmem()...]
    all_gather x4 -> x0, waiting for transfers between devices: 128 us -> none  [the longest x1 56.7 us: body(): lax.all_gather(ffn_out.astype(jnp.bfloat16), 'shard', axis=1, tiled=True)]
    unnamed x6 -> x0, waiting for transfers between devices: 124 us -> none
    reshape x10 -> x3, local copies, waits for them, and re-layouts: 107 us -> 0.16 us  [the longest x1 0.08 us: body(): jnp.stack(vec_sums, axis=1).reshape(-1)]
    dot_general x66 -> x0, matrix products: 92 us -> none  [the longest x14 28.9 us: contract_rows(): lax.dot_general(left_side, right_side, (((0,), (0,)), ((), ())), preferre...]
  transfers between devices with their start and end apart: 5 -> 56, of which waited for: 4 -> 29; matrix products, arithmetic and copies ran while one was open for 4% -> 13% of each run, Pallas kernels for 0% -> 17%
where the time goes in v1:
time: 466 us; the launch traced here: 456 us
  waiting for transfers between devices  161 us (35%)
  Pallas kernels  153 us (33%)
  starting transfers between devices  52 us (11%)
  local copies, waits for them, and re-layouts  46 us (10%)
  other arithmetic  42.2 us (9%)
    ppermute x56, waiting for transfers between devices, swap(): return lax.ppermute(values, axis, [(i, i ^ 1 << bit) for i in range(count)])  161 us
    pallas_call x7, Pallas kernels, call(): pl.pallas_call(kernel, out_shape=outs, in_specs=specs, out_specs=[vmem()...  97.7 us
    ppermute x56, starting transfers between devices, swap(): return lax.ppermute(values, axis, [(i, i ^ 1 << bit) for i in range(count)])  52 us
    pallas_call x2, Pallas kernels, update_ffn(): pl.pallas_call(kernel, out_shape=[shape(dims, f32) for dims in outs] + [s...  36.5 us
    pallas_call x1, Pallas kernels, update_rest(): pl.pallas_call(kernel, out_shape=[shape(attn[0].shape, f32)] * 3 + [shape...  18.5 us
    sub x6, other arithmetic, move(): return weight - LEARN_RATE * factor * update  14 us
    unnamed x85, local copies, waits for them, and re-layouts  12.4 us
  transfers between devices with their start and end apart: 56, of which 29 were waited for; matrix products, arithmetic and copies ran while one was open for 13% of the time, Pallas kernels for 17%

profile of v1, /device:TPU:0, one launch (start us, length us, event | category | flops | bytes accessed | tf_op | source)
XLA Modules:
  0.0 456.4 jit_solution(15841725820546284823)
XLA Ops:
  4.4 4.1 fusion.9
  9.3 4.5 fusion.8
  23.7 20.4 %collective-permute-done.7.rest_1_ = bf16[128,1536]{1,0:T(8,128)(2,1)} collective-permute-done((bf16[128,1536]{1,0:T(8,128)(2,1)}, bf16[128,1536]{1,0:T(8,128)(2,1)}, u32[]{:S(2)}, u32[]{:S(2)}) %collective-permute-start.7) | collective-permute-done | bytes 393248 | tf_op jit(solution)/shard_map/ppermute | solution.py:118
  48.2 7.1 %collective-permute-done.5.rest_1_ = bf16[4,128,512]{2,1,0:T(8,128)(2,1)} collective-permute-done((bf16[4,128,512]{2,1,0:T(8,128)(2,1)}, bf16[4,128,512]{2,1,0:T(8,128)(2,1)}, u32[]{:S(2)}, u32[]{:S(2)}) %collective-permute-start.5) | collective-permute-done | bytes 524320 | tf_op jit(solution)/shard_map/ppermute | solution.py:118
  56.6 10.0 %collective-permute-done.9.rest_1_ = bf16[128,2048]{1,0:T(8,128)(2,1)} collective-permute-done((bf16[128,2048]{1,0:T(8,128)(2,1)}, bf16[128,2048]{1,0:T(8,128)(2,1)}, u32[]{:S(2)}, u32[]{:S(2)}) %collective-permute-start.9) | collective-permute-done | bytes 524320 | tf_op jit(solution)/shard_map/ppermute | solution.py:118
  66.6 9.8 %collective-permute-done.11.rest_4_ = bf16[512,512]{1,0:T(8,128)(2,1)} collective-permute-done((bf16[512,512]{1,0:T(8,128)(2,1)S(1)}, bf16[512,512]{1,0:T(8,128)(2,1)}, u32[]{:S(2)}, u32[]{:S(2)}) %collective-permute-start.11) | collective-permute-done | bytes 524320 | tf_op jit(solution)/shard_map/ppermute | solution.py:118
  76.9 8.1 %ffn_first.1 = (f32[512,512]{1,0:T(8,128)}, bf16[512,512]{1,0:T(8,128)(2,1)}, bf16[512,2048]{1,0:T(8,128)(2,1)}, bf16[512,2048]{1,0:T(8,128)(2,1)}) custom-call(s32[3]{0:T(128)} %pad_add_fusion.place_ref, bf16[512,512]{1,0:T(8,128)(2,1)} %bitcast.50, f32[40,512]{1,0:T(8,128)} %pad_convert_fusion.vec_ref, bf16[256,2048]{1,0:T(8,128)(2,1)} %get-tuple-element.193.rest_0_, ...), custom_call_target="tpu_custom_call" | custom-call | flops 2147483648 | bytes 12000000 | tf_op jit(solution)/shard_map/ffn_first/pallas_call | solution.py:192
  85.9 14.3 %attend.1 = (f32[512,512]{1,0:T(8,128)}, bf16[512,512]{1,0:T(8,128)(2,1)}, bf16[3,4,512,128]{3,2,1,0:T(8,128)(2,1)}, bf16[16,256,256]{2,1,0:T(8,128)(2,1)}, bf16[512,512]{1,0:T(8,128)(2,1)}) custom-call(s32[3]{0:T(128)} %pad_add_fusion.place_ref, s32[2]{0:T(128)} %len_ref.3, f32[512,512]{1,0:T(8,128)} %get-tuple-element.86.x_ref, ...), custom_call_target="tpu_custom_call" | custom-call | flops 2147483648 | bytes 20000000 | tf_op jit(solution)/shard_map/attend/pallas_call | solution.py:192
  100.9 8.1 %convolve.1 = (f32[512,512]{1,0:T(8,128)}, bf16[512,512]{1,0:T(8,128)(2,1)}, f32[2,4,288,128]{3,2,1,0:T(8,128)}, f32[512,512]{1,0:T(8,128)}, f32[512,512]{1,0:T(8,128)}, /*index=5*/bf16[512,512]{1,0:T(8,128)(2,1)}) custom-call(s32[3]{0:T(128)} %pad_add_fusion.place_ref, f32[512,512]{1,0:T(8,128)} %get-tuple-element.87.x_ref, ...), custom_call_target="tpu_custom_call" | custom-call | flops 1610612736 | bytes 16000000 | tf_op jit(solution)/shard_map/convolve/pallas_call | solution.py:192
  110.1 13.8 %ffn_last.1 = (bf16[512,512]{1,0:T(8,128)(2,1)}, f32[512,512]{1,0:T(8,128)}, f32[8,512]{1,0:T(8,128)}, bf16[32,128,512]{2,1,0:T(8,128)(2,1)}) custom-call(s32[3]{0:T(128)} %pad_add_fusion.place_ref, s32[2]{0:T(128)} %len_ref.3, f32[512,512]{1,0:T(8,128)} %get-tuple-element.88.x_ref, f32[40,512]{1,0:T(8,128)} %pad_convert_fusion.vec_ref, ...), custom_call_target="tpu_custom_call" | custom-call | flops 6442450944 | bytes 16000000 | tf_op jit(solution)/shard_map/ffn_last/pallas_call | solution.py:192
  123.8 18.7 %convolve_back.1 = (f32[512,512]{1,0:T(8,128)}, f32[8,512]{1,0:T(8,128)}, f32[32,512]{1,0:T(8,128)}, bf16[32,48,512]{2,1,0:T(8,128)(2,1)}) custom-call(s32[3]{0:T(128)} %pad_add_fusion.place_ref, f32[512,512]{1,0:T(8,128)} %get-tuple-element.90.grad_ref, f32[512,512]{1,0:T(8,128)} %get-tuple-element.87.x_ref, f32[40,512]{1,0:T(8,128)} %pad_convert_fusion.vec_ref, ...), custom_call_target="tpu_custom_call" | custom-call | flops 5368709120 | bytes 20000000 | tf_op jit(solution)/shard_map/convolve_back/pallas_call | solution.py:192
  142.6 23.1 %attend_back.1 = (f32[512,512]{1,0:T(8,128)}, f32[8,512]{1,0:T(8,128)}, f32[512,128]{1,0:T(8,128)}, bf16[32,64,512]{2,1,0:T(8,128)(2,1)}) custom-call(s32[3]{0:T(128)} %pad_add_fusion.place_ref, f32[512,512]{1,0:T(8,128)} %get-tuple-element.96.grad_ref, f32[512,512]{1,0:T(8,128)} %get-tuple-element.86.x_ref, f32[40,512]{1,0:T(8,128)} %pad_convert_fusion.vec_ref, ...), custom_call_target="tpu_custom_call" | custom-call | flops 6710886400 | bytes 24000000 | tf_op jit(solution)/shard_map/attend_back/pallas_call | solution.py:192
  167.9 11.6 %ffn_first_back.1 = (bf16[512,512]{1,0:T(8,128)(2,1)}, f32[8,512]{1,0:T(8,128)}, bf16[32,128,512]{2,1,0:T(8,128)(2,1)}) custom-call(s32[3]{0:T(128)} %pad_add_fusion.place_ref, f32[512,512]{1,0:T(8,128)} %get-tuple-element.101.grad_ref, bf16[512,512]{1,0:T(8,128)(2,1)} %bitcast.51, f32[40,512]{1,0:T(8,128)} %pad_convert_fusion.vec_ref, ...), custom_call_target="tpu_custom_call" | custom-call | flops 4294967296 | bytes 16000000 | tf_op jit(solution)/shard_map/ffn_first_back/pallas_call | solution.py:192
  184.8 4.8 %collective-permute-done.32 = f32[48,512]{1,0:T(8,128)S(1)} collective-permute-done((f32[48,512]{1,0:T(8,128)S(1)}, f32[48,512]{1,0:T(8,128)S(1)}, u32[]{:S(2)}, u32[]{:S(2)}) %collective-permute-start.32) | collective-permute-done | bytes 98336 | tf_op jit(solution)/shard_map/ppermute | solution.py:118
  202.5 3.2 slice.266
  215.4 6.9 %collective-permute-done.47 = bf16[8,48,512]{2,1,0:T(8,128)(2,1)} collective-permute-done((bf16[8,48,512]{2,1,0:T(8,128)(2,1)S(1)}, bf16[8,48,512]{2,1,0:T(8,128)(2,1)}, u32[]{:S(2)}, u32[]{:S(2)}) %collective-permute-start.47) | collective-permute-done | bytes 393248 | tf_op jit(solution)/shard_map/ppermute | solution.py:118
  245.4 6.1 %collective-permute-done.38 = bf16[8,64,512]{2,1,0:T(8,128)(2,1)S(1)} collective-permute-done((bf16[8,64,512]{2,1,0:T(8,128)(2,1)S(1)}, bf16[8,64,512]{2,1,0:T(8,128)(2,1)S(1)}, u32[]{:S(2)}, u32[]{:S(2)}) %collective-permute-start.38) | collective-permute-done | bytes 524320 | tf_op jit(solution)/shard_map/ppermute | solution.py:118
  260.3 13.6 %collective-permute-done.23 = bf16[8,128,512]{2,1,0:T(8,128)(2,1)S(1)} collective-permute-done((bf16[8,128,512]{2,1,0:T(8,128)(2,1)S(1)}, bf16[8,128,512]{2,1,0:T(8,128)(2,1)S(1)}, u32[]{:S(2)}, u32[]{:S(2)}) %collective-permute-start.23) | collective-permute-done | bytes 1048608 | tf_op jit(solution)/shard_map/ppermute | solution.py:118
  275.9 16.6 %collective-permute-done.14 = bf16[8,128,512]{2,1,0:T(8,128)(2,1)S(1)} collective-permute-done((bf16[8,128,512]{2,1,0:T(8,128)(2,1)S(1)}, bf16[8,128,512]{2,1,0:T(8,128)(2,1)S(1)}, u32[]{:S(2)}, u32[]{:S(2)}) %collective-permute-start.14) | collective-permute-done | bytes 1048608 | tf_op jit(solution)/shard_map/ppermute | solution.py:118
  298.7 4.2 collective-permute-done.15
  308.0 7.4 %collective-permute-done.16 = bf16[2,128,512]{2,1,0:T(8,128)(2,1)S(1)} collective-permute-done((bf16[2,128,512]{2,1,0:T(8,128)(2,1)S(1)}, bf16[2,128,512]{2,1,0:T(8,128)(2,1)S(1)}, u32[]{:S(2)}, u32[]{:S(2)}) %collective-permute-start.16) | collective-permute-done | bytes 262176 | tf_op jit(solution)/shard_map/ppermute | solution.py:118
  318.6 6.6 %collective-permute-done.17 = bf16[1,128,512]{2,1,0:T(8,128)(2,1)S(1)} collective-permute-done((bf16[1,128,512]{2,1,0:T(8,128)(2,1)S(1)}, bf16[1,128,512]{2,1,0:T(8,128)(2,1)S(1)}, u32[]{:S(2)}, u32[]{:S(2)}) %collective-permute-start.17) | collective-permute-done | bytes 131104 | tf_op jit(solution)/shard_map/ppermute | solution.py:118
  325.9 3.7 collective-permute-start.43
  337.2 4.5 collective-permute-done.28
  342.8 3.6 collective-permute-done.19
  348.4 8.2 %collective-permute-done.29 = bf16[4,128,512]{2,1,0:T(8,128)(2,1)S(1)} collective-permute-done((bf16[4,128,512]{2,1,0:T(8,128)(2,1)S(1)}, bf16[4,128,512]{2,1,0:T(8,128)(2,1)S(1)}, u32[]{:S(2)}, u32[]{:S(2)}) %collective-permute-start.29) | collective-permute-done | bytes 524320 | tf_op jit(solution)/shard_map/ppermute | solution.py:118
  357.7 7.6 %collective-permute-done.20 = bf16[4,128,512]{2,1,0:T(8,128)(2,1)S(1)} collective-permute-done((bf16[4,128,512]{2,1,0:T(8,128)(2,1)S(1)}, bf16[4,128,512]{2,1,0:T(8,128)(2,1)S(1)}, u32[]{:S(2)}, u32[]{:S(2)}) %collective-permute-start.20) | collective-permute-done | bytes 524320 | tf_op jit(solution)/shard_map/ppermute | solution.py:118
  368.0 18.5 %update_rest.1 = (f32[4,256,512]{2,1,0:T(8,128)}, f32[4,256,512]{2,1,0:T(8,128)}, f32[4,256,512]{2,1,0:T(8,128)}, f32[3,256,512]{2,1,0:T(8,128)}, f32[256,512]{1...) custom-call(s32[16]{0:T(128)} %broadcast_xor_fusion.spot_ref, ...), custom_call_target="tpu_custom_call" | custom-call | bytes 28000000 | tf_op jit(solution)/shard_map/update_rest/pallas_call | solution.py:773
  391.4 18.2 %update_ffn.2 = (f32[2,256,2048]{2,1,0:T(8,128)}, f32[2,256,2048]{2,1,0:T(8,128)}, f32[2,256,2048]{2,1,0:T(8,128)}, f32[2,256,2048]{2,1,0:T(8,128)}, f32[2,1024,...) custom-call(s32[16]{0:T(128)} %broadcast_xor_fusion.spot_ref, ...), custom_call_target="tpu_custom_call" | custom-call | bytes 32000000 | tf_op jit(solution)/shard_map/update_ffn/pallas_call | solution.py:711
  411.9 18.4 %update_ffn.3 = (f32[2,256,2048]{2,1,0:T(8,128)}, f32[2,256,2048]{2,1,0:T(8,128)}, f32[2,256,2048]{2,1,0:T(8,128)}, f32[2,256,2048]{2,1,0:T(8,128)}, f32[2,1024,...) custom-call(s32[16]{0:T(128)} %broadcast_xor_fusion.spot_ref, ...), custom_call_target="tpu_custom_call", output_to_operand_aliasing={{0}: (8, {}), {1}: (9, {}), {2}: (10, {}), {3}: (11, {}), {... | custom-call | bytes 32000000 | tf_op jit(solution)/shard_map/update_ffn/pallas_call | solution.py:711
  439.4 6.9 %multiply_subtract_fusion.1 = f32[2,256,2048]{2,1,0:T(8,128)} fusion(f32[2,256,2048]{2,1,0:T(8,128)} %w0.3, f32[2,256,2048]{2,1,0:T(8,128)} %get-tuple-element.128, f32[2]{0:T(128)S(1)} %get-tuple-element.207), kind=kLoop, calls=%fused_computation.1 | loop fusion | flops 2097152 | bytes 12582920 | tf_op jit(solution)/shard_map/sub | solution.py:800
  446.3 3.1 multiply_subtract_fusion
  (312 shorter events, 138.0 us)
Async XLA Ops:
  1.5 22.2 %collective-permute-start = (bf16[37,256]{1,0:T(8,128)(2,1)S(1)}, bf16[37,256]{1,0:T(8,128)(2,1)S(1)}, u32[]{:S(2)}, u32[]{:S(2)}) collective-permute-start(bf16[37,256]{1,0:T(8,128)(2,1)S(1)} %convert_element_type.245), channel_id=1, source_target_pairs={{0,1},{1,0},{2,3},{3,2},{4,5},{5,4},{6,7},{7,6},{8,9},{9,8},{10,11... | collective-permute-start | bytes 56840 | tf_op jit(solution)/shard_map/ppermute | solution.py:118
  9.3 34.8 %collective-permute-start.1 = (bf16[128,2048]{1,0:T(8,128)(2,1)}, bf16[128,2048]{1,0:T(8,128)(2,1)}, u32[]{:S(2)}, u32[]{:S(2)}) collective-permute-start(bf16[128,2048]{1,0:T(8,128)(2,1)} %fusion), channel_id=1, source_target_pairs={{0,1},{1,0},{2,3},{3,2},{4,5},{5,4},{6,7},{7,6},{8,9},{9,8},{10,11... | collective-permute-start | bytes 1572872 | tf_op jit(solution)/shard_map/ppermute | solution.py:118
  15.8 28.3 %collective-permute-start.3 = (bf16[512,512]{1,0:T(8,128)(2,1)}, bf16[512,512]{1,0:T(8,128)(2,1)}, u32[]{:S(2)}, u32[]{:S(2)}) collective-permute-start(bf16[512,512]{1,0:T(8,128)(2,1)} %fusion.1), channel_id=1, source_target_pairs={{0,1},{1,0},{2,3},{3,2},{4,5},{5,4},{6,7},{7,6},{8,9},{9,8},{10,11... | collective-permute-start | bytes 1572872 | tf_op jit(solution)/shard_map/ppermute | solution.py:118
  19.8 24.3 %collective-permute-start.7 = (bf16[128,1536]{1,0:T(8,128)(2,1)}, bf16[128,1536]{1,0:T(8,128)(2,1)}, u32[]{:S(2)}, u32[]{:S(2)}) collective-permute-start(bf16[128,1536]{1,0:T(8,128)(2,1)} %dynamic-slice_convert_fusion.5), channel_id=1, source_target_pairs={{0,1},{1,0},{2,3},{3,2},{4,5},{5,4},{6,7},{7,6},{8,9},{9,8},{10,11... | collective-permute-start | bytes 1179656 | tf_op jit(solution)/shard_map/ppermute | solution.py:118
  20.6 34.7 %collective-permute-start.5 = (bf16[4,128,512]{2,1,0:T(8,128)(2,1)}, bf16[4,128,512]{2,1,0:T(8,128)(2,1)}, u32[]{:S(2)}, u32[]{:S(2)}) collective-permute-start(bf16[4,128,512]{2,1,0:T(8,128)(2,1)} %dynamic-slice_convert_fusion.2), channel_id=1, source_target_pairs={{0,1},{1,0},{2,3},{3,2},{4,5},{5,4},{6,7},{7,6},{8,9},{9,8},{10,11... | collective-permute-start | bytes 1572872 | tf_op jit(solution)/shard_map/ppermute | solution.py:118
  23.6 42.9 %collective-permute-start.9 = (bf16[128,2048]{1,0:T(8,128)(2,1)}, bf16[128,2048]{1,0:T(8,128)(2,1)}, u32[]{:S(2)}, u32[]{:S(2)}) collective-permute-start(bf16[128,2048]{1,0:T(8,128)(2,1)} %fusion.2), channel_id=1, source_target_pairs={{0,1},{1,0},{2,3},{3,2},{4,5},{5,4},{6,7},{7,6},{8,9},{9,8},{10,11... | collective-permute-start | bytes 1572872 | tf_op jit(solution)/shard_map/ppermute | solution.py:118
  44.1 32.3 %collective-permute-start.11 = (bf16[512,512]{1,0:T(8,128)(2,1)S(1)}, bf16[512,512]{1,0:T(8,128)(2,1)}, u32[]{:S(2)}, u32[]{:S(2)}) collective-permute-start(bf16[512,512]{1,0:T(8,128)(2,1)S(1)} %fusion.3), channel_id=1, source_target_pairs={{0,1},{1,0},{2,3},{3,2},{4,5},{5,4},{6,7},{7,6},{8,9},{9,8},{10,11... | collective-permute-start | bytes 1572872 | tf_op jit(solution)/shard_map/ppermute | solution.py:118
  44.1 32.3 %collective-permute-start.2 = (bf16[128,2048]{1,0:T(8,128)(2,1)}, bf16[128,2048]{1,0:T(8,128)(2,1)}, u32[]{:S(2)}, u32[]{:S(2)}) collective-permute-start(bf16[128,2048]{1,0:T(8,128)(2,1)} %collective-permute-done.1.rest_1_), channel_id=1, source_target_pairs={{0,2},{2,0},{4,6},{6,4},{8,10},{10,8},{12,14},{14,12},{16,18},{18,... | collective-permute-start | bytes 1572872 | tf_op jit(solution)/shard_map/ppermute | solution.py:118
  44.1 32.8 %collective-permute-start.4 = (bf16[512,512]{1,0:T(8,128)(2,1)}, bf16[512,512]{1,0:T(8,128)(2,1)}, u32[]{:S(2)}, u32[]{:S(2)}) collective-permute-start(bf16[512,512]{1,0:T(8,128)(2,1)} %collective-permute-done.3.rest_4_), channel_id=1, source_target_pairs={{0,2},{2,0},{4,6},{6,4},{8,10},{10,8},{12,14},{14,12},{16,18},{18,... | collective-permute-start | bytes 1572872 | tf_op jit(solution)/shard_map/ppermute | solution.py:118
  55.3 29.7 %collective-permute-start.6 = (bf16[4,128,512]{2,1,0:T(8,128)(2,1)}, bf16[4,128,512]{2,1,0:T(8,128)(2,1)S(1)}, u32[]{:S(2)}, u32[]{:S(2)}) collective-permute-start(bf16[4,128,512]{2,1,0:T(8,128)(2,1)} %collective-permute-done.5.rest_1_), channel_id=1, source_target_pairs={{0,2},{2,0},{4,6},{6,4},{8,10},{10,8},{12,14},{14,12},{16,18},{18,... | collective-permute-start | bytes 1572872 | tf_op jit(solution)/shard_map/ppermute | solution.py:118
  66.6 33.6 %collective-permute-start.8 = (bf16[128,1536]{1,0:T(8,128)(2,1)}, bf16[128,1536]{1,0:T(8,128)(2,1)S(1)}, u32[]{:S(2)}, u32[]{:S(2)}) collective-permute-start(bf16[128,1536]{1,0:T(8,128)(2,1)} %collective-permute-done.7.rest_1_), channel_id=1, source_target_pairs={{0,2},{2,0},{4,6},{6,4},{8,10},{10,8},{12,14},{14,12},{16,18},{18,... | collective-permute-start | bytes 1179656 | tf_op jit(solution)/shard_map/ppermute | solution.py:118
  76.4 32.7 %collective-permute-start.10 = (bf16[128,2048]{1,0:T(8,128)(2,1)}, bf16[128,2048]{1,0:T(8,128)(2,1)S(1)}, u32[]{:S(2)}, u32[]{:S(2)}) collective-permute-start(bf16[128,2048]{1,0:T(8,128)(2,1)} %collective-permute-done.9.rest_1_), channel_id=1, source_target_pairs={{0,2},{2,0},{4,6},{6,4},{8,10},{10,8},{12,14},{14,12},{16,18},{18,... | collective-permute-start | bytes 1572872 | tf_op jit(solution)/shard_map/ppermute | solution.py:118
  76.4 32.7 %collective-permute-start.12 = (bf16[512,512]{1,0:T(8,128)(2,1)}, bf16[512,512]{1,0:T(8,128)(2,1)S(1)}, u32[]{:S(2)}, u32[]{:S(2)}) collective-permute-start(bf16[512,512]{1,0:T(8,128)(2,1)} %collective-permute-done.11.rest_4_), channel_id=1, source_target_pairs={{0,2},{2,0},{4,6},{6,4},{8,10},{10,8},{12,14},{14,12},{16,18},{18,... | collective-permute-start | bytes 1572872 | tf_op jit(solution)/shard_map/ppermute | solution.py:118
  167.9 41.9 %collective-permute-start.46 = (bf16[16,48,512]{2,1,0:T(8,128)(2,1)}, bf16[16,48,512]{2,1,0:T(8,128)(2,1)}, u32[]{:S(2)}, u32[]{:S(2)}) collective-permute-start(bf16[16,48,512]{2,1,0:T(8,128)(2,1)} %slice.313), channel_id=1, source_target_pairs={{0,2},{2,0},{4,6},{6,4},{8,10},{10,8},{12,14},{14,12},{16,18},{18,... | collective-permute-start | bytes 2359304 | tf_op jit(solution)/shard_map/ppermute | solution.py:118
  205.7 38.2 %collective-permute-start.13 = (bf16[16,128,512]{2,1,0:T(8,128)(2,1)}, bf16[16,128,512]{2,1,0:T(8,128)(2,1)S(1)}, u32[]{:S(2)}, u32[]{:S(2)}) collective-permute-start(bf16[16,128,512]{2,1,0:T(8,128)(2,1)} %slice.266), channel_id=1, source_target_pairs={{0,2},{2,0},{4,6},{6,4},{8,10},{10,8},{12,14},{14,12},{16,18},{18,... | collective-permute-start | bytes 6291464 | tf_op jit(solution)/shard_map/ppermute | solution.py:118
  207.3 32.6 %collective-permute-start.22 = (bf16[16,128,512]{2,1,0:T(8,128)(2,1)}, bf16[16,128,512]{2,1,0:T(8,128)(2,1)}, u32[]{:S(2)}, u32[]{:S(2)}) collective-permute-start(bf16[16,128,512]{2,1,0:T(8,128)(2,1)} %slice.276), channel_id=1, source_target_pairs={{0,2},{2,0},{4,6},{6,4},{8,10},{10,8},{12,14},{14,12},{16,18},{18,... | collective-permute-start | bytes 6291464 | tf_op jit(solution)/shard_map/ppermute | solution.py:118
  209.2 25.3 %collective-permute-start.37 = (bf16[16,64,512]{2,1,0:T(8,128)(2,1)}, bf16[16,64,512]{2,1,0:T(8,128)(2,1)}, u32[]{:S(2)}, u32[]{:S(2)}) collective-permute-start(bf16[16,64,512]{2,1,0:T(8,128)(2,1)} %slice.303), channel_id=1, source_target_pairs={{0,2},{2,0},{4,6},{6,4},{8,10},{10,8},{12,14},{14,12},{16,18},{18,... | collective-permute-start | bytes 3145736 | tf_op jit(solution)/shard_map/ppermute | solution.py:118
  236.6 14.9 %collective-permute-start.38 = (bf16[8,64,512]{2,1,0:T(8,128)(2,1)S(1)}, bf16[8,64,512]{2,1,0:T(8,128)(2,1)S(1)}, u32[]{:S(2)}, u32[]{:S(2)}) collective-permute-start(bf16[8,64,512]{2,1,0:T(8,128)(2,1)S(1)} %slice.365), channel_id=1, source_target_pairs={{0,1},{1,0},{2,3},{3,2},{4,5},{5,4},{6,7},{7,6},{8,9},{9,8},{10,11... | collective-permute-start | bytes 1572872 | tf_op jit(solution)/shard_map/ppermute | solution.py:118
  239.8 13.4 %collective-permute-start.51 = (bf16[1,48,512]{2,1,0:T(8,128)(2,1)S(1)}, bf16[1,48,512]{2,1,0:T(8,128)(2,1)S(1)}, u32[]{:S(2)}, u32[]{:S(2)}) collective-permute-start(bf16[1,48,512]{2,1,0:T(8,128)(2,1)S(1)} %get-tuple-element.178), channel_id=1, source_target_pairs={{0,16},{2,18},{4,20},{6,22},{8,24},{10,26},{12,28},{14,30},{16,0},... | collective-permute-start | bytes 147464 | tf_op jit(solution)/shard_map/ppermute | solution.py:118
  242.4 31.5 %collective-permute-start.23 = (bf16[8,128,512]{2,1,0:T(8,128)(2,1)S(1)}, bf16[8,128,512]{2,1,0:T(8,128)(2,1)S(1)}, u32[]{:S(2)}, u32[]{:S(2)}) collective-permute-start(bf16[8,128,512]{2,1,0:T(8,128)(2,1)S(1)} %slice.353), channel_id=1, source_target_pairs={{0,1},{1,0},{2,3},{3,2},{4,5},{5,4},{6,7},{7,6},{8,9},{9,8},{10,11... | collective-permute-start | bytes 3145736 | tf_op jit(solution)/shard_map/ppermute | solution.py:118
  244.8 47.7 %collective-permute-start.14 = (bf16[8,128,512]{2,1,0:T(8,128)(2,1)S(1)}, bf16[8,128,512]{2,1,0:T(8,128)(2,1)S(1)}, u32[]{:S(2)}, u32[]{:S(2)}) collective-permute-start(bf16[8,128,512]{2,1,0:T(8,128)(2,1)S(1)} %slice.345), channel_id=1, source_target_pairs={{0,1},{1,0},{2,3},{3,2},{4,5},{5,4},{6,7},{7,6},{8,9},{9,8},{10,11... | collective-permute-start | bytes 3145736 | tf_op jit(solution)/shard_map/ppermute | solution.py:118
  257.9 36.5 %collective-permute-start.53 = (bf16[4,48,512]{2,1,0:T(8,128)(2,1)S(1)}, bf16[4,48,512]{2,1,0:T(8,128)(2,1)S(1)}, u32[]{:S(2)}, u32[]{:S(2)}) collective-permute-start(bf16[4,48,512]{2,1,0:T(8,128)(2,1)S(1)} %pad_maximum_fusion.9), channel_id=1, source_target_pairs={{0,4},{2,6},{4,0},{6,2},{8,12},{10,14},{12,8},{14,10},{16,20},{18,... | collective-permute-start | bytes 589832 | tf_op jit(solution)/shard_map/ppermute | solution.py:118
  258.6 35.9 %collective-permute-start.40 = (bf16[2,64,512]{2,1,0:T(8,128)(2,1)S(1)}, bf16[2,64,512]{2,1,0:T(8,128)(2,1)S(1)}, u32[]{:S(2)}, u32[]{:S(2)}) collective-permute-start(bf16[2,64,512]{2,1,0:T(8,128)(2,1)S(1)} %slice.369), channel_id=1, source_target_pairs={{0,8},{2,10},{4,12},{6,14},{8,0},{10,2},{12,4},{14,6},{16,24},{18,... | collective-permute-start | bytes 393224 | tf_op jit(solution)/shard_map/ppermute | solution.py:118
  274.3 22.9 %collective-permute-start.24 = (bf16[4,128,512]{2,1,0:T(8,128)(2,1)S(1)}, bf16[4,128,512]{2,1,0:T(8,128)(2,1)S(1)}, u32[]{:S(2)}, u32[]{:S(2)}) collective-permute-start(bf16[4,128,512]{2,1,0:T(8,128)(2,1)S(1)} %slice.355), channel_id=1, source_target_pairs={{0,4},{2,6},{4,0},{6,2},{8,12},{10,14},{12,8},{14,10},{16,20},{18,... | collective-permute-start | bytes 1572872 | tf_op jit(solution)/shard_map/ppermute | solution.py:118
  294.5 53.9 %collective-permute-start.54 = (bf16[8,48,512]{2,1,0:T(8,128)(2,1)S(1)}, bf16[8,48,512]{2,1,0:T(8,128)(2,1)S(1)}, u32[]{:S(2)}, u32[]{:S(2)}) collective-permute-start(bf16[8,48,512]{2,1,0:T(8,128)(2,1)S(1)} %pad_maximum_fusion.5), channel_id=1, source_target_pairs={{0,2},{2,0},{4,6},{6,4},{8,10},{10,8},{12,14},{14,12},{16,18},{18,... | collective-permute-start | bytes 1179656 | tf_op jit(solution)/shard_map/ppermute | solution.py:118
  304.9 20.9 %collective-permute-start.42 = (bf16[1,64,512]{2,1,0:T(8,128)(2,1)S(1)}, bf16[1,64,512]{2,1,0:T(8,128)(2,1)S(1)}, u32[]{:S(2)}, u32[]{:S(2)}) collective-permute-start(bf16[1,64,512]{2,1,0:T(8,128)(2,1)S(1)} %get-tuple-element.180), channel_id=1, source_target_pairs={{0,16},{2,18},{4,20},{6,22},{8,24},{10,26},{12,28},{14,30},{16,0},... | collective-permute-start | bytes 196616 | tf_op jit(solution)/shard_map/ppermute | solution.py:118
  317.2 12.5 %collective-permute-start.27 = (bf16[1,128,512]{2,1,0:T(8,128)(2,1)S(1)}, bf16[1,128,512]{2,1,0:T(8,128)(2,1)S(1)}, u32[]{:S(2)}, u32[]{:S(2)}) collective-permute-start(bf16[1,128,512]{2,1,0:T(8,128)(2,1)S(1)} %get-tuple-element.185), channel_id=1, source_target_pairs={{0,16},{2,18},{4,20},{6,22},{8,24},{10,26},{12,28},{14,30},{16,0},... | collective-permute-start | bytes 393224 | tf_op jit(solution)/shard_map/ppermute | solution.py:118
  341.8 14.9 %collective-permute-start.29 = (bf16[4,128,512]{2,1,0:T(8,128)(2,1)S(1)}, bf16[4,128,512]{2,1,0:T(8,128)(2,1)S(1)}, u32[]{:S(2)}, u32[]{:S(2)}) collective-permute-start(bf16[4,128,512]{2,1,0:T(8,128)(2,1)S(1)} %pad_maximum_fusion.3), channel_id=1, source_target_pairs={{0,4},{2,6},{4,0},{6,2},{8,12},{10,14},{12,8},{14,10},{16,20},{18,... | collective-permute-start | bytes 1572872 | tf_op jit(solution)/shard_map/ppermute | solution.py:118
  346.5 18.8 %collective-permute-start.20 = (bf16[4,128,512]{2,1,0:T(8,128)(2,1)S(1)}, bf16[4,128,512]{2,1,0:T(8,128)(2,1)S(1)}, u32[]{:S(2)}, u32[]{:S(2)}) collective-permute-start(bf16[4,128,512]{2,1,0:T(8,128)(2,1)S(1)} %pad_maximum_fusion.2), channel_id=1, source_target_pairs={{0,4},{2,6},{4,0},{6,2},{8,12},{10,14},{12,8},{14,10},{16,20},{18,... | collective-permute-start | bytes 1572872 | tf_op jit(solution)/shard_map/ppermute | solution.py:118
  347.6 19.5 %collective-permute-start.45 = (bf16[8,64,512]{2,1,0:T(8,128)(2,1)S(1)}, bf16[8,64,512]{2,1,0:T(8,128)(2,1)S(1)}, u32[]{:S(2)}, u32[]{:S(2)}) collective-permute-start(bf16[8,64,512]{2,1,0:T(8,128)(2,1)S(1)} %pad_maximum_fusion.4), channel_id=1, source_target_pairs={{0,2},{2,0},{4,6},{6,4},{8,10},{10,8},{12,14},{14,12},{16,18},{18,... | collective-permute-start | bytes 1572872 | tf_op jit(solution)/shard_map/ppermute | solution.py:118
  357.7 31.1 %collective-permute-start.30 = (bf16[8,128,512]{2,1,0:T(8,128)(2,1)}, bf16[8,128,512]{2,1,0:T(8,128)(2,1)}, u32[]{:S(2)}, u32[]{:S(2)}) collective-permute-start(bf16[8,128,512]{2,1,0:T(8,128)(2,1)} %pad_maximum_fusion.1), channel_id=1, source_target_pairs={{0,2},{2,0},{4,6},{6,4},{8,10},{10,8},{12,14},{14,12},{16,18},{18,... | collective-permute-start | bytes 3145736 | tf_op jit(solution)/shard_map/ppermute | solution.py:118
  366.4 43.2 %collective-permute-start.21 = (bf16[8,128,512]{2,1,0:T(8,128)(2,1)}, bf16[8,128,512]{2,1,0:T(8,128)(2,1)}, u32[]{:S(2)}, u32[]{:S(2)}) collective-permute-start(bf16[8,128,512]{2,1,0:T(8,128)(2,1)} %pad_maximum_fusion), channel_id=1, source_target_pairs={{0,2},{2,0},{4,6},{6,4},{8,10},{10,8},{12,14},{14,12},{16,18},{18,... | collective-permute-start | bytes 3145736 | tf_op jit(solution)/shard_map/ppermute | solution.py:118
  (57 other events, 462.0 us)
